TPU v7x, 32 devices: a whole 2x2x4 slice. The times are simulated.
32 devices in a mesh: dp: 8 (over z, core), tensor: 4 (over y, x).
Axes of the slice: x: 2, y: 2, z: 4, core: 2. Of those that a mesh axis runs over, the one named last changes fastest.
Arguments:
- tokens: bfloat16 [24576, 1536], P(('dp', 'tensor')), may hold values from -6 to 6
- cotangent: bfloat16 [24576, 1536], P(('dp', 'tensor')), may hold values from -6 to 6
- seg_ids: int32 [8, 3072], P('dp'), may hold values from 0 to 3, never falling along the last dimension, each value on 1 to 2048 neighbouring positions
- gain_attn: bfloat16 [1536], P('dp'), may hold values from 0.5 to 1.5
- gain_ffn: bfloat16 [1536], P('dp'), may hold values from 0.5 to 1.5
- w_query: bfloat16 [1536, 1536], P('dp', 'tensor'), may hold values from -0.17860863 to 0.17860863
- w_key: bfloat16 [1536, 768], P('dp', 'tensor'), may hold values from -0.17860863 to 0.17860863
- value_projection: bfloat16 [1536, 768], P('dp', 'tensor'), may hold values from -0.15625 to 0.15625
- w_out: bfloat16 [1536, 1536], P('tensor', 'dp'), may hold values from -0.625 to 0.625
- w_gate: bfloat16 [1536, 4096], P('dp', 'tensor'), may hold values from -0.15625 to 0.15625
- w_up: bfloat16 [1536, 4096], P('dp', 'tensor'), may hold values from -0.15625 to 0.15625
- w_down: bfloat16 [4096, 1536], P('tensor', 'dp'), may hold values from -0.09375 to 0.09375
Outputs:
- layer_out: bfloat16 [24576, 1536], P(('dp', 'tensor'))
- grad_tokens: float32 [24576, 1536], P(('dp', 'tensor'))
- grad_gain_attn: float32 [1536], P('dp')
- grad_gain_ffn: float32 [1536], P('dp')
- grad_query: float32 [1536, 1536], P('dp', 'tensor')
- grad_key: float32 [1536, 768], P('dp', 'tensor')
- grad_value: float32 [1536, 768], P('dp', 'tensor')
- grad_out: float32 [1536, 1536], P('tensor', 'dp')
- grad_gate: float32 [1536, 4096], P('dp', 'tensor')
- grad_up: float32 [1536, 4096], P('dp', 'tensor')
- grad_down: float32 [4096, 1536], P('tensor', 'dp')
Inputs may be any that keep to these rules, and one draw needn't show every extreme that they name: `seg_ids`: in each pack the values never fall along the tokens; each of the 4 sequences has 1 to 2048 tokens, and one of them exactly 2048.
All inputs are finite; a program needn't handle non-finite values.
Results may differ from a plain program's by a relative error of at most 0.02.
Values may be sent and summed in bfloat16 or wider, within the bound.
No kernel may reach another device: no remote copies, remote signals or barrier semaphores. Data moves between devices by JAX's collectives and lax.ppermute only.
A program may use at most 256 MiB of HBM per device.

v0:
```python
import jax
import jax.numpy as jnp
from jax import lax
from jax.sharding import PartitionSpec as P

QUERY_HEADS = 16
KEY_VALUE_HEADS = 8
HEAD_SIZE = 96
SEGS = 4


rope_base = 100000.0
small_eps = 1e-05
masked_value = -1e30


def matrix_product(left, right):
    return jnp.dot(left, right, preferred_element_type=jnp.float32)


def dot_rows(left, right):
    return lax.dot_general(
        left, right, (((0,), (0,)), ((), ())), preferred_element_type=jnp.float32
    )


def dot_cols(left, right):
    return lax.dot_general(
        left, right, (((1,), (1,)), ((), ())), preferred_element_type=jnp.float32
    )


def positions(segment_ids):
    length_axis = segment_ids.shape[-1]
    labels = jnp.arange(SEGS, dtype=jnp.int32)
    member = (segment_ids[..., :, None] == labels).astype(jnp.int32)
    lengths_of = jnp.sum(member, axis=-2)
    earlier = (labels < segment_ids[..., :, None]).astype(jnp.int32)
    first_row = jnp.sum(earlier * lengths_of[..., None, :], axis=-1)
    return jnp.arange(length_axis, dtype=jnp.int32) - first_row


def angles_of(position_ids):
    frequency = rope_base ** (-jnp.arange(HEAD_SIZE // 2, dtype=jnp.float32) * 2.0 / HEAD_SIZE)
    phase_angle = position_ids.astype(jnp.float32)[..., None] * frequency
    return (jnp.cos(phase_angle), jnp.sin(phase_angle))


def rotate(values, cosine, sine_table):
    half_width = values.shape[-1] // 2
    front_half = values[..., :half_width]
    back_half = values[..., half_width:]
    return jnp.concatenate(
        [
            front_half * cosine - back_half * sine_table,
            back_half * cosine + front_half * sine_table,
        ],
        axis=-1,
    )


def unrotate(values, cosine, sine_table):
    half_width = values.shape[-1] // 2
    front_half = values[..., :half_width]
    back_half = values[..., half_width:]
    return jnp.concatenate(
        [
            front_half * cosine + back_half * sine_table,
            back_half * cosine - front_half * sine_table,
        ],
        axis=-1,
    )


def rms_scale(hidden):
    return lax.rsqrt(jnp.mean(hidden * hidden, axis=-1, keepdims=True) + small_eps)


def norm_back(grad_normed, normed, inverse, gain):
    scaled = grad_normed * gain
    return inverse * (scaled - normed * jnp.mean(scaled * normed, axis=-1, keepdims=True))


def on_device(
    tokens,
    cotangent,
    seg_ids,
    gain_attn,
    gain_ffn,
    w_query,
    w_key,
    value_projection,
    w_out,
    w_gate,
    w_up,
    w_down,
):
    gathered = (
        lax.all_gather(gain_attn, "dp", axis=0, tiled=True),
        lax.all_gather(gain_ffn, "dp", axis=0, tiled=True),
        lax.all_gather(w_query, "dp", axis=0, tiled=True),
        lax.all_gather(w_key, "dp", axis=0, tiled=True),
        lax.all_gather(value_projection, "dp", axis=0, tiled=True),
        lax.all_gather(w_out, "dp", axis=1, tiled=True),
        lax.all_gather(w_gate, "dp", axis=0, tiled=True),
        lax.all_gather(w_up, "dp", axis=0, tiled=True),
        lax.all_gather(w_down, "dp", axis=1, tiled=True),
    )
    gain_one = gathered[0].astype(jnp.float32)
    gain_two = gathered[1].astype(jnp.float32)
    query_weight, key_weight, value_weight, out_weight, gate_weight, up_weight, down_weight = (
        gathered[2:]
    )
    segment_row = seg_ids[0]
    pack_rows = segment_row.shape[0]
    kv_local = key_weight.shape[1] // HEAD_SIZE
    group_width = QUERY_HEADS // KEY_VALUE_HEADS
    heads_local = kv_local * group_width
    cosine, sine_table = angles_of(positions(segment_row))
    cosine_heads = cosine[:, None, None, :]
    sine_heads = sine_table[:, None, None, :]
    cosine_keys = cosine[:, None, :]
    sine_keys = sine_table[:, None, :]
    hidden_in = tokens.astype(jnp.float32)
    inverse_one = rms_scale(hidden_in)
    normed_one = hidden_in * inverse_one
    attention_input = (normed_one * gain_one).astype(jnp.bfloat16)
    attn_rows = lax.all_gather(attention_input, "tensor", axis=0, tiled=True)
    query_lin = matrix_product(attn_rows, query_weight).reshape(
        pack_rows, kv_local, group_width, HEAD_SIZE
    )
    query_rot = rotate(query_lin, cosine_heads, sine_heads).astype(jnp.bfloat16)
    key_linear = matrix_product(attn_rows, key_weight).reshape(pack_rows, kv_local, HEAD_SIZE)
    key_rot = rotate(key_linear, cosine_keys, sine_keys).astype(jnp.bfloat16)
    rows_of_values = (
        matrix_product(attn_rows, value_weight)
        .astype(jnp.bfloat16)
        .reshape(pack_rows, kv_local, HEAD_SIZE)
    )
    rows_of_block = min(512, pack_rows)
    block_list = pack_rows // rows_of_block
    score_scale = HEAD_SIZE ** (-0.5)
    key_index = jnp.arange(pack_rows, dtype=jnp.int32)
    begins = jnp.arange(block_list, dtype=jnp.int32) * rows_of_block

    def block_scores(begin_row):
        query_block = lax.dynamic_slice_in_dim(query_rot, begin_row, rows_of_block, 0)
        raw_scores = jnp.einsum(
            "qcgd,kcd->cgqk", query_block, key_rot, preferred_element_type=jnp.float32
        )
        scores = raw_scores * score_scale
        query_index = begin_row + jnp.arange(rows_of_block, dtype=jnp.int32)
        query_segment = lax.dynamic_slice_in_dim(segment_row, begin_row, rows_of_block)
        allowed = (query_segment[:, None] == segment_row[None, :]) & (
            key_index[None, :] <= query_index[:, None]
        )
        return (query_block, jnp.where(allowed, scores, masked_value))

    def forward_block(begin_row):
        query_block, scores = block_scores(begin_row)
        largest = jnp.max(scores, axis=-1, keepdims=True)
        exp_scores = jnp.exp(scores - largest)
        row_total = jnp.sum(exp_scores, axis=-1, keepdims=True)
        softmax_rows = (exp_scores / row_total).astype(jnp.bfloat16)
        attended = jnp.einsum(
            "cgqk,kcd->qcgd", softmax_rows, rows_of_values, preferred_element_type=jnp.float32
        )
        return (attended.astype(jnp.bfloat16), largest[..., 0] + jnp.log(row_total[..., 0]))

    attn_blocks, log_totals = lax.map(forward_block, begins)
    attn_out = attn_blocks.reshape(pack_rows, heads_local * HEAD_SIZE)
    branch = lax.psum_scatter(
        matrix_product(attn_out, out_weight), "tensor", scatter_dimension=0, tiled=True
    )
    hidden_mid = hidden_in + branch
    inverse_two = rms_scale(hidden_mid)
    normed_two = hidden_mid * inverse_two
    ffn_input = (normed_two * gain_two).astype(jnp.bfloat16)
    cotangent_full = cotangent.astype(jnp.float32)
    ffn_rows = lax.all_gather(ffn_input, "tensor", axis=0, tiled=True)
    gate_lin = matrix_product(ffn_rows, gate_weight)
    up_lin = matrix_product(ffn_rows, up_weight)
    gate_sigmoid = jax.nn.sigmoid(gate_lin)
    gate_act = gate_lin * gate_sigmoid
    units_out = (gate_act * up_lin).astype(jnp.bfloat16)
    result = (
        hidden_mid
        + lax.psum_scatter(
            matrix_product(units_out, down_weight).astype(jnp.bfloat16),
            "tensor",
            scatter_dimension=0,
            tiled=True,
        ).astype(jnp.float32)
    ).astype(jnp.bfloat16)
    cotangent_rows = lax.all_gather(cotangent, "tensor", axis=0, tiled=True)
    grad_units = dot_cols(cotangent_rows, down_weight)
    grad_gate_lin = (
        grad_units * up_lin * gate_sigmoid * (1.0 + gate_lin * (1.0 - gate_sigmoid))
    ).astype(jnp.bfloat16)
    grad_up_lin = (grad_units * gate_act).astype(jnp.bfloat16)
    grad_gate_w = dot_rows(ffn_rows, grad_gate_lin)
    grad_up_w = dot_rows(ffn_rows, grad_up_lin)
    grad_down_w = dot_rows(units_out, cotangent_rows)
    grad_ffn_input = lax.psum_scatter(
        dot_cols(grad_gate_lin, gate_weight) + dot_cols(grad_up_lin, up_weight),
        "tensor",
        scatter_dimension=0,
        tiled=True,
    )
    grad_mid = cotangent_full + norm_back(grad_ffn_input, normed_two, inverse_two, gain_two)
    gain_two_part = jnp.sum(grad_ffn_input * normed_two, axis=0)
    grad_branch = grad_mid.astype(jnp.bfloat16)
    branch_rows = lax.all_gather(grad_branch, "tensor", axis=0, tiled=True)
    grad_out_w = dot_rows(attn_out, branch_rows)
    grad_attended = (
        dot_cols(branch_rows, out_weight)
        .astype(jnp.bfloat16)
        .reshape(pack_rows, kv_local, group_width, HEAD_SIZE)
    )

    def backward_block(running, begin_row):
        key_grad, value_grad = running
        query_block, scores = block_scores(begin_row)
        log_block = lax.dynamic_index_in_dim(
            log_totals, begin_row // rows_of_block, 0, keepdims=False
        )
        softmax_rows = jnp.exp(scores - log_block[..., None])
        grad_block = lax.dynamic_slice_in_dim(grad_attended, begin_row, rows_of_block, 0)
        grad_soft = jnp.einsum(
            "qcgd,kcd->cgqk", grad_block, rows_of_values, preferred_element_type=jnp.float32
        )
        row_inner = jnp.sum(softmax_rows * grad_soft, axis=-1, keepdims=True)
        grad_raw = (softmax_rows * (grad_soft - row_inner) * score_scale).astype(jnp.bfloat16)
        query_grad = jnp.einsum(
            "cgqk,kcd->qcgd", grad_raw, key_rot, preferred_element_type=jnp.float32
        )
        key_grad = key_grad + jnp.einsum(
            "cgqk,qcgd->kcd", grad_raw, query_block, preferred_element_type=jnp.float32
        )
        value_grad = value_grad + jnp.einsum(
            "cgqk,qcgd->kcd",
            softmax_rows.astype(jnp.bfloat16),
            grad_block,
            preferred_element_type=jnp.float32,
        )
        return ((key_grad, value_grad), query_grad)

    zero_keys = jnp.zeros((pack_rows, kv_local, HEAD_SIZE), jnp.float32)
    (key_grad, value_grad), query_grads = lax.scan(backward_block, (zero_keys, zero_keys), begins)
    query_grad = unrotate(
        query_grads.reshape(pack_rows, kv_local, group_width, HEAD_SIZE), cosine_heads, sine_heads
    )
    query_grad = query_grad.astype(jnp.bfloat16).reshape(pack_rows, heads_local * HEAD_SIZE)
    key_grad_low = (
        unrotate(key_grad, cosine_keys, sine_keys)
        .astype(jnp.bfloat16)
        .reshape(pack_rows, kv_local * HEAD_SIZE)
    )
    value_grad_low = value_grad.astype(jnp.bfloat16).reshape(pack_rows, kv_local * HEAD_SIZE)
    grad_query_w = dot_rows(attn_rows, query_grad)
    grad_key_w = dot_rows(attn_rows, key_grad_low)
    grad_value_w = dot_rows(attn_rows, value_grad_low)
    grad_attn_input = lax.psum_scatter(
        (
            dot_cols(query_grad, query_weight)
            + dot_cols(key_grad_low, key_weight)
            + dot_cols(value_grad_low, value_weight)
        ).astype(jnp.bfloat16),
        "tensor",
        scatter_dimension=0,
        tiled=True,
    ).astype(jnp.float32)
    grad_tokens = grad_mid + norm_back(grad_attn_input, normed_one, inverse_one, gain_one)
    gain_one_part = jnp.sum(grad_attn_input * normed_one, axis=0)
    gain_one_sum, gain_two_sum = lax.psum((gain_one_part, gain_two_part), "tensor")
    reduced = (
        lax.psum_scatter(
            gain_one_sum.astype(jnp.bfloat16), "dp", scatter_dimension=0, tiled=True
        ).astype(jnp.float32),
        lax.psum_scatter(
            gain_two_sum.astype(jnp.bfloat16), "dp", scatter_dimension=0, tiled=True
        ).astype(jnp.float32),
        lax.psum_scatter(
            grad_query_w.astype(jnp.bfloat16), "dp", scatter_dimension=0, tiled=True
        ).astype(jnp.float32),
        lax.psum_scatter(
            grad_key_w.astype(jnp.bfloat16), "dp", scatter_dimension=0, tiled=True
        ).astype(jnp.float32),
        lax.psum_scatter(
            grad_value_w.astype(jnp.bfloat16), "dp", scatter_dimension=0, tiled=True
        ).astype(jnp.float32),
        lax.psum_scatter(
            grad_out_w.astype(jnp.bfloat16), "dp", scatter_dimension=1, tiled=True
        ).astype(jnp.float32),
        lax.psum_scatter(
            grad_gate_w.astype(jnp.bfloat16), "dp", scatter_dimension=0, tiled=True
        ).astype(jnp.float32),
        lax.psum_scatter(
            grad_up_w.astype(jnp.bfloat16), "dp", scatter_dimension=0, tiled=True
        ).astype(jnp.float32),
        lax.psum_scatter(
            grad_down_w.astype(jnp.bfloat16), "dp", scatter_dimension=1, tiled=True
        ).astype(jnp.float32),
    )
    return (
        result,
        grad_tokens,
        reduced[0],
        reduced[1],
        reduced[2],
        reduced[3],
        reduced[4],
        reduced[5],
        reduced[6],
        reduced[7],
        reduced[8],
    )


def solution(mesh):
    return jax.shard_map(
        on_device,
        mesh=mesh,
        in_specs=(
            P(("dp", "tensor"), None),
            P(("dp", "tensor"), None),
            P("dp", None),
            P("dp"),
            P("dp"),
            P("dp", "tensor"),
            P("dp", "tensor"),
            P("dp", "tensor"),
            P("tensor", "dp"),
            P("dp", "tensor"),
            P("dp", "tensor"),
            P("tensor", "dp"),
        ),
        out_specs=(
            P(("dp", "tensor"), None),
            P(("dp", "tensor"), None),
            P("dp"),
            P("dp"),
            P("dp", "tensor"),
            P("dp", "tensor"),
            P("dp", "tensor"),
            P("tensor", "dp"),
            P("dp", "tensor"),
            P("dp", "tensor"),
            P("tensor", "dp"),
        ),
        check_vma=False,
    )
```

profile of v0, /device:TPU:0, one launch (start us, length us, event | category | flops | bytes accessed | tf_op | source)
XLA Modules:
  0.0 2449.5 jit_solution(15019305134644403800)
XLA Ops:
  13.2 18.9 all-reduce.6
  72.6 58.4 %all-gather.10.cloned.1.call-done = bf16[3072,1536]{1,0:T(8,128)(2,1)} async-done(((bf16[768,1536]{1,0:T(8,128)(2,1)}), bf16[3072,1536]{1,0:T(8,128)(2,1)}) %all-gather.10.cloned.1.call-update) | async-done | bytes 9437200 | tf_op jit(solution)/shard_map/all_gather | solution.py:128
  138.3 17.2 all-gather.12.cloned.1.call-done
  171.5 254.6 %while.30 = (s32[]{:T(128)}, bf16[6,512,2,2,96]{1,4,3,2,0:T(8,128)(2,1)}, f32[6,2,2,512]{3,2,1,0:T(2,128)}, s32[6]{0:T(128)S(1)}, s32[3072]{0:T(1024)S(1)}, /*in...) while((s32[]{:T(128)}, ...), condition=%wide.region_6.7_spmd.clone, body=%wide.region_3.6_spmd.clone.sunk | while | flops 2496330240 | bytes 85022904 | solution.py:170
  444.5 170.0 %reduce-scatter.12.cloned.1.call-done = f32[768,1536]{1,0:T(8,128)} async-done(((f32[3072,1536]{1,0:T(8,128)}), f32[768,1536]{1,0:T(8,128)}) %reduce-scatter.12.cloned.1.call-update) | async-done | bytes 4718608 | tf_op jit(solution)/shard_map/reduce_scatter | solution.py:172
  623.9 30.3 %all-gather.20.cloned.1.call-done = bf16[1536,1024]{1,0:T(8,128)(2,1)} async-done(((bf16[192,1024]{1,0:T(8,128)(2,1)}), bf16[1536,1024]{1,0:T(8,128)(2,1)}) %all-gather.20.cloned.1.call-update) | async-done | bytes 3145744 | tf_op jit(solution)/shard_map/all_gather | solution.py:106
  654.2 97.4 %all-gather.16.cloned.1.call-done = bf16[3072,1536]{1,0:T(8,128)(2,1)} async-done(((bf16[768,1536]{1,0:T(8,128)(2,1)}), bf16[3072,1536]{1,0:T(8,128)(2,1)}) %all-gather.16.cloned.1.call-update) | async-done | bytes 9437200 | tf_op jit(solution)/shard_map/all_gather | solution.py:180
  768.0 23.6 all-gather.18.cloned.1.call-done
  807.7 22.7 all-gather.22.cloned.1.call-done
  830.3 97.0 %all-gather.24.cloned.1.call-done = bf16[3072,1536]{1,0:T(8,128)(2,1)} async-done(((bf16[768,1536]{1,0:T(8,128)(2,1)}), bf16[3072,1536]{1,0:T(8,128)(2,1)}) %all-gather.24.cloned.1.call-update) | async-done | bytes 9437200 | tf_op jit(solution)/shard_map/all_gather | solution.py:195
  927.3 24.0 multiply_convert_fusion
  951.3 18.4 fusion.84
  969.7 20.8 convolution_add_fusion
  990.6 170.9 %reduce-scatter.16.cloned.1.call-done = f32[768,1536]{1,0:T(8,128)} async-done(((f32[3072,1536]{1,0:T(8,128)}), f32[768,1536]{1,0:T(8,128)}) %reduce-scatter.16.cloned.1.call-update) | async-done | bytes 4718608 | tf_op jit(solution)/shard_map/reduce_scatter | solution.py:204
  1219.7 48.8 %all-gather.26.cloned.1.call-done = bf16[3072,1536]{1,0:T(8,128)(2,1)} async-done(((bf16[768,1536]{1,0:T(8,128)(2,1)}), bf16[3072,1536]{1,0:T(8,128)(2,1)}) %all-gather.26.cloned.1.call-update) | async-done | bytes 9437200 | tf_op jit(solution)/shard_map/all_gather | solution.py:213
  1282.7 814.3 %while.31 = (s32[]{:T(128)}, f32[3072,2,96]{0,2,1:T(8,128)}, f32[3072,2,96]{0,2,1:T(8,128)}, f32[6,512,2,2,96]{1,0,4,3,2:T(8,128)}, s32[6]{0:T(128)S(1)}, /*inde...) while((s32[]{:T(128)}, f32[3072,2,96]{0,2,1:T(8,128)}, ...), condition=%wide.region_14.15_spmd.clone, body=%wide.region_12.14_spmd.clone.sunk | while | flops 6210464256 | bytes 257628624 | solution.py:249
  1327.6 35.7 %fusion.164 = f32[1,512,2,2,96]{1,4,3,2,0:T(8,128)} fusion(f32[2,512,2,3072]{3,1,2,0:T(8,128)} %fusion.159, f32[2,512,2,3072]{3,1,2,0:T(8,128)} %fusion.160, f32[2,2,512]{2,1,0:T(2,128)S(1)} %dynamic-slice_bitcast_fusion.2, pred[512,3072]{1,0:T(8,128)(4,1)S(1)} %fusion.161, bf16[3072,2,96]{0,2,1:T(8,128)(2,1)S(1)} %get-tuple-element.583), kind=kOutput, calls=%fused_computation.43.clone.1 | convolution fusion | flops 1277170688 | bytes 53878784 | tf_op jit(solution)/shard_map/while/body/eval_jaxpr/cgqk,kcd->qcgd/dot_general | solution.py:234
  1363.3 37.5 %fusion.162 = f32[3072,2,96]{0,2,1:T(8,128)} fusion(f32[2,512,2,3072]{3,1,2,0:T(8,128)} %fusion.159, f32[2,512,2,3072]{3,1,2,0:T(8,128)} %fusion.160, f32[2,2,512]{2,1,0:T(2,128)S(1)} %dynamic-slice_bitcast_fusion.2, pred[512,3072]{1,0:T(8,128)(4,1)S(1)} %fusion.161, f32[3072,2,96]{0,2,1:T(8,128)} %get-tuple-element.557, pred[]{:T(512)S(6)} %compare.7, ...), kind=kOutput, calls=%fused_computation.42.clone.1 | convolution fusion | flops 1278350336 | bytes 108937224 | tf_op jit(solution)/shard_map/while/body/eval_jaxpr/cgqk,qcgd->kcd/dot_general | solution.py:237
  1463.8 35.0 %fusion.164 = f32[1,512,2,2,96]{1,4,3,2,0:T(8,128)} fusion(f32[2,512,2,3072]{3,1,2,0:T(8,128)} %fusion.159, f32[2,512,2,3072]{3,1,2,0:T(8,128)} %fusion.160, f32[2,2,512]{2,1,0:T(2,128)S(1)} %dynamic-slice_bitcast_fusion.2, pred[512,3072]{1,0:T(8,128)(4,1)S(1)} %fusion.161, bf16[3072,2,96]{0,2,1:T(8,128)(2,1)S(1)} %get-tuple-element.583), kind=kOutput, calls=%fused_computation.43.clone.1 | convolution fusion | flops 1277170688 | bytes 53878784 | tf_op jit(solution)/shard_map/while/body/eval_jaxpr/cgqk,kcd->qcgd/dot_general | solution.py:234
  1498.8 37.5 %fusion.162 = f32[3072,2,96]{0,2,1:T(8,128)} fusion(f32[2,512,2,3072]{3,1,2,0:T(8,128)} %fusion.159, f32[2,512,2,3072]{3,1,2,0:T(8,128)} %fusion.160, f32[2,2,512]{2,1,0:T(2,128)S(1)} %dynamic-slice_bitcast_fusion.2, pred[512,3072]{1,0:T(8,128)(4,1)S(1)} %fusion.161, f32[3072,2,96]{0,2,1:T(8,128)} %get-tuple-element.557, pred[]{:T(512)S(6)} %compare.7, ...), kind=kOutput, calls=%fused_computation.42.clone.1 | convolution fusion | flops 1278350336 | bytes 108937224 | tf_op jit(solution)/shard_map/while/body/eval_jaxpr/cgqk,qcgd->kcd/dot_general | solution.py:237
  1599.2 35.0 %fusion.164 = f32[1,512,2,2,96]{1,4,3,2,0:T(8,128)} fusion(f32[2,512,2,3072]{3,1,2,0:T(8,128)} %fusion.159, f32[2,512,2,3072]{3,1,2,0:T(8,128)} %fusion.160, f32[2,2,512]{2,1,0:T(2,128)S(1)} %dynamic-slice_bitcast_fusion.2, pred[512,3072]{1,0:T(8,128)(4,1)S(1)} %fusion.161, bf16[3072,2,96]{0,2,1:T(8,128)(2,1)S(1)} %get-tuple-element.583), kind=kOutput, calls=%fused_computation.43.clone.1 | convolution fusion | flops 1277170688 | bytes 53878784 | tf_op jit(solution)/shard_map/while/body/eval_jaxpr/cgqk,kcd->qcgd/dot_general | solution.py:234
  1634.3 37.5 %fusion.162 = f32[3072,2,96]{0,2,1:T(8,128)} fusion(f32[2,512,2,3072]{3,1,2,0:T(8,128)} %fusion.159, f32[2,512,2,3072]{3,1,2,0:T(8,128)} %fusion.160, f32[2,2,512]{2,1,0:T(2,128)S(1)} %dynamic-slice_bitcast_fusion.2, pred[512,3072]{1,0:T(8,128)(4,1)S(1)} %fusion.161, f32[3072,2,96]{0,2,1:T(8,128)} %get-tuple-element.557, pred[]{:T(512)S(6)} %compare.7, ...), kind=kOutput, calls=%fused_computation.42.clone.1 | convolution fusion | flops 1278350336 | bytes 108937224 | tf_op jit(solution)/shard_map/while/body/eval_jaxpr/cgqk,qcgd->kcd/dot_general | solution.py:237
  1734.7 35.0 %fusion.164 = f32[1,512,2,2,96]{1,4,3,2,0:T(8,128)} fusion(f32[2,512,2,3072]{3,1,2,0:T(8,128)} %fusion.159, f32[2,512,2,3072]{3,1,2,0:T(8,128)} %fusion.160, f32[2,2,512]{2,1,0:T(2,128)S(1)} %dynamic-slice_bitcast_fusion.2, pred[512,3072]{1,0:T(8,128)(4,1)S(1)} %fusion.161, bf16[3072,2,96]{0,2,1:T(8,128)(2,1)S(1)} %get-tuple-element.583), kind=kOutput, calls=%fused_computation.43.clone.1 | convolution fusion | flops 1277170688 | bytes 53878784 | tf_op jit(solution)/shard_map/while/body/eval_jaxpr/cgqk,kcd->qcgd/dot_general | solution.py:234
  1769.7 37.7 %fusion.162 = f32[3072,2,96]{0,2,1:T(8,128)} fusion(f32[2,512,2,3072]{3,1,2,0:T(8,128)} %fusion.159, f32[2,512,2,3072]{3,1,2,0:T(8,128)} %fusion.160, f32[2,2,512]{2,1,0:T(2,128)S(1)} %dynamic-slice_bitcast_fusion.2, pred[512,3072]{1,0:T(8,128)(4,1)S(1)} %fusion.161, f32[3072,2,96]{0,2,1:T(8,128)} %get-tuple-element.557, pred[]{:T(512)S(6)} %compare.7, ...), kind=kOutput, calls=%fused_computation.42.clone.1 | convolution fusion | flops 1278350336 | bytes 108937224 | tf_op jit(solution)/shard_map/while/body/eval_jaxpr/cgqk,qcgd->kcd/dot_general | solution.py:237
  1870.3 35.0 %fusion.164 = f32[1,512,2,2,96]{1,4,3,2,0:T(8,128)} fusion(f32[2,512,2,3072]{3,1,2,0:T(8,128)} %fusion.159, f32[2,512,2,3072]{3,1,2,0:T(8,128)} %fusion.160, f32[2,2,512]{2,1,0:T(2,128)S(1)} %dynamic-slice_bitcast_fusion.2, pred[512,3072]{1,0:T(8,128)(4,1)S(1)} %fusion.161, bf16[3072,2,96]{0,2,1:T(8,128)(2,1)S(1)} %get-tuple-element.583), kind=kOutput, calls=%fused_computation.43.clone.1 | convolution fusion | flops 1277170688 | bytes 53878784 | tf_op jit(solution)/shard_map/while/body/eval_jaxpr/cgqk,kcd->qcgd/dot_general | solution.py:234
  1905.4 37.5 %fusion.162 = f32[3072,2,96]{0,2,1:T(8,128)} fusion(f32[2,512,2,3072]{3,1,2,0:T(8,128)} %fusion.159, f32[2,512,2,3072]{3,1,2,0:T(8,128)} %fusion.160, f32[2,2,512]{2,1,0:T(2,128)S(1)} %dynamic-slice_bitcast_fusion.2, pred[512,3072]{1,0:T(8,128)(4,1)S(1)} %fusion.161, f32[3072,2,96]{0,2,1:T(8,128)} %get-tuple-element.557, pred[]{:T(512)S(6)} %compare.7, ...), kind=kOutput, calls=%fused_computation.42.clone.1 | convolution fusion | flops 1278350336 | bytes 108937224 | tf_op jit(solution)/shard_map/while/body/eval_jaxpr/cgqk,qcgd->kcd/dot_general | solution.py:237
  2005.8 35.0 %fusion.164 = f32[1,512,2,2,96]{1,4,3,2,0:T(8,128)} fusion(f32[2,512,2,3072]{3,1,2,0:T(8,128)} %fusion.159, f32[2,512,2,3072]{3,1,2,0:T(8,128)} %fusion.160, f32[2,2,512]{2,1,0:T(2,128)S(1)} %dynamic-slice_bitcast_fusion.2, pred[512,3072]{1,0:T(8,128)(4,1)S(1)} %fusion.161, bf16[3072,2,96]{0,2,1:T(8,128)(2,1)S(1)} %get-tuple-element.583), kind=kOutput, calls=%fused_computation.43.clone.1 | convolution fusion | flops 1277170688 | bytes 53878784 | tf_op jit(solution)/shard_map/while/body/eval_jaxpr/cgqk,kcd->qcgd/dot_general | solution.py:234
  2040.8 37.5 %fusion.162 = f32[3072,2,96]{0,2,1:T(8,128)} fusion(f32[2,512,2,3072]{3,1,2,0:T(8,128)} %fusion.159, f32[2,512,2,3072]{3,1,2,0:T(8,128)} %fusion.160, f32[2,2,512]{2,1,0:T(2,128)S(1)} %dynamic-slice_bitcast_fusion.2, pred[512,3072]{1,0:T(8,128)(4,1)S(1)} %fusion.161, f32[3072,2,96]{0,2,1:T(8,128)} %get-tuple-element.557, pred[]{:T(512)S(6)} %compare.7, ...), kind=kOutput, calls=%fused_computation.42.clone.1 | convolution fusion | flops 1278350336 | bytes 108937224 | tf_op jit(solution)/shard_map/while/body/eval_jaxpr/cgqk,qcgd->kcd/dot_general | solution.py:237
  2166.1 17.4 add_convert_fusion
  2212.3 26.7 %reduce-scatter.20.cloned.1.call-done = bf16[192,384]{1,0:T(8,128)(2,1)} async-done(((bf16[1536,384]{1,0:T(8,128)(2,1)}), bf16[192,384]{1,0:T(8,128)(2,1)}) %reduce-scatter.20.cloned.1.call-update) | async-done | bytes 147472 | tf_op jit(solution)/shard_map/reduce_scatter | solution.py:283
  2240.7 94.5 %reduce-scatter.18.cloned.1.call-done = bf16[768,1536]{1,0:T(8,128)(2,1)} async-done(((bf16[3072,1536]{1,0:T(8,128)(2,1)}), bf16[768,1536]{1,0:T(8,128)(2,1)}) %reduce-scatter.18.cloned.1.call-update) | async-done | bytes 2359312 | tf_op jit(solution)/shard_map/reduce_scatter | solution.py:263
  2368.7 64.7 %reduce-scatter.14.cloned.1.call-done = bf16[768,1536]{1,0:T(8,128)(2,1)} async-done(((bf16[3072,1536]{1,0:T(8,128)(2,1)}), bf16[768,1536]{1,0:T(8,128)(2,1)}) %reduce-scatter.14.cloned.1.call-update) | async-done | bytes 2359312 | tf_op jit(solution)/shard_map/reduce_scatter | solution.py:188
  (324 shorter events, 938.9 us)
Async XLA Ops:
  7.2 123.8 %all-gather.10.cloned.1.call-start = ((), (), s32[]{:S(2)}) async-start(), calls=%async_computation.11 | async-start | bytes 11796480 | tf_op jit(solution)/shard_map/all_gather | solution.py:128
  36.4 119.0 %all-gather.12.cloned.1.call-start = ((), (), s32[]{:S(2)}) async-start(), calls=%async_computation.12 | async-start | bytes 1327104 | tf_op jit(solution)/shard_map/all_gather | solution.py:101
  37.2 395.4 %all-gather.14.cloned.1.call-start = ((), (), s32[]{:S(2)}) async-start(), calls=%async_computation.13 | async-start | bytes 1327104 | tf_op jit(solution)/shard_map/all_gather | solution.py:104
  37.9 576.6 %reduce-scatter.12.cloned.1.call-start = ((), (), s32[]{:S(2)}) async-start(), calls=%async_computation.14 | async-start | bytes 23592960 | tf_op jit(solution)/shard_map/reduce_scatter | solution.py:172
  70.5 94.2 %copy-start.20 = (bf16[1536,192]{1,0:T(8,128)(2,1)}, bf16[1536,192]{1,0:T(8,128)(2,1)S(1)}, u32[]{:S(2)}) copy-start(bf16[1536,192]{1,0:T(8,128)(2,1)S(1)} %all_gather.43) | copy-start | bytes 1769476
  443.8 170.7 %copy-start.1 = (bf16[768,1536]{1,0:T(8,128)(2,1)S(1)}, bf16[768,1536]{1,0:T(8,128)(2,1)}, u32[]{:S(2)}) copy-start(bf16[768,1536]{1,0:T(8,128)(2,1)} %param.16) | copy-start | bytes 7077892
  443.8 210.4 %all-gather.20.cloned.1.call-start = ((), (), s32[]{:S(2)}) async-start(), calls=%async_computation.17 | async-start | bytes 3538944 | tf_op jit(solution)/shard_map/all_gather | solution.py:106
  444.4 307.3 %all-gather.16.cloned.1.call-start = ((), (), s32[]{:S(2)}) async-start(), calls=%async_computation.15 | async-start | bytes 11796480 | tf_op jit(solution)/shard_map/all_gather | solution.py:180
  444.5 722.7 %copy-start.25 = (f32[1536]{0:T(1024)}, f32[1536]{0:T(1024)S(1)}, u32[]{:S(2)}) copy-start(f32[1536]{0:T(1024)S(1)} %convert_element_type.158) | copy-start | bytes 18436
  617.6 549.6 %copy-start.29 = (f32[768]{0:T(1024)}, f32[768]{0:T(1024)S(1)}, u32[]{:S(2)}) copy-start(f32[768]{0:T(1024)S(1)} %add_rsqrt_fusion) | copy-start | bytes 9220
  621.6 169.9 %all-gather.18.cloned.1.call-start = ((), (), s32[]{:S(2)}) async-start(), calls=%async_computation.16 | async-start | bytes 3538944 | tf_op jit(solution)/shard_map/all_gather | solution.py:105
  622.4 208.0 %all-gather.22.cloned.1.call-start = ((), (), s32[]{:S(2)}) async-start(), calls=%async_computation.18 | async-start | bytes 3538944 | tf_op jit(solution)/shard_map/all_gather | solution.py:107
  623.1 304.2 %all-gather.24.cloned.1.call-start = ((), (), s32[]{:S(2)}) async-start(), calls=%async_computation.20 | async-start | bytes 11796480 | tf_op jit(solution)/shard_map/all_gather | solution.py:195
  623.8 537.6 %reduce-scatter.16.cloned.1.call-start = ((), (), s32[]{:S(2)}) async-start(), calls=%async_computation.21 | async-start | bytes 23592960 | tf_op jit(solution)/shard_map/reduce_scatter | solution.py:204
  990.5 177.2 %copy-start.8 = (bf16[768,1536]{1,0:T(8,128)(2,1)S(1)}, bf16[768,1536]{1,0:T(8,128)(2,1)}, u32[]{:S(2)}) copy-start(bf16[768,1536]{1,0:T(8,128)(2,1)} %param.17) | copy-start | bytes 7077892
  990.6 277.9 %all-gather.26.cloned.1.call-start = ((), (), s32[]{:S(2)}) async-start(), calls=%async_computation.22 | async-start | bytes 11796480 | tf_op jit(solution)/shard_map/all_gather | solution.py:213
  1172.1 1029.5 %reduce-scatter.32.cloned.1.call-start = ((), (), s32[]{:S(2)}) async-start(), calls=%async_computation.30 | async-start | bytes 3538944 | tf_op jit(solution)/shard_map/reduce_scatter | solution.py:301
  1188.1 1015.5 %reduce-scatter.30.cloned.1.call-start = ((), (), s32[]{:S(2)}) async-start(), calls=%async_computation.29 | async-start | bytes 3538944 | tf_op jit(solution)/shard_map/reduce_scatter | solution.py:298
  1203.8 1001.7 %reduce-scatter.28.cloned.1.call-start = ((), (), s32[]{:S(2)}) async-start(), calls=%async_computation.28 | async-start | bytes 3538944 | tf_op jit(solution)/shard_map/reduce_scatter | solution.py:295
  1219.6 987.9 %reduce-scatter.22.cloned.1.call-start = ((), (), s32[]{:S(2)}) async-start(), calls=%async_computation.25 | async-start | bytes 884736 | tf_op jit(solution)/shard_map/reduce_scatter | solution.py:286
  2107.8 101.3 %reduce-scatter.24.cloned.1.call-start = ((), (), s32[]{:S(2)}) async-start(), calls=%async_computation.26 | async-start | bytes 884736 | tf_op jit(solution)/shard_map/reduce_scatter | solution.py:289
  2125.8 84.8 %reduce-scatter.26.cloned.1.call-start = ((), (), s32[]{:S(2)}) async-start(), calls=%async_computation.27 | async-start | bytes 1327104 | tf_op jit(solution)/shard_map/reduce_scatter | solution.py:292
  2134.8 104.2 %reduce-scatter.20.cloned.1.call-start = ((), (), s32[]{:S(2)}) async-start(), calls=%async_computation.24 | async-start | bytes 1327104 | tf_op jit(solution)/shard_map/reduce_scatter | solution.py:283
  2147.3 187.9 %reduce-scatter.18.cloned.1.call-start = ((), (), s32[]{:S(2)}) async-start(), calls=%async_computation.23 | async-start | bytes 11796480 | tf_op jit(solution)/shard_map/reduce_scatter | solution.py:263
  2183.6 249.7 %reduce-scatter.14.cloned.1.call-start = ((), (), s32[]{:S(2)}) async-start(), calls=%async_computation.19 | async-start | bytes 11796480 | tf_op jit(solution)/shard_map/reduce_scatter | solution.py:188
  2200.7 134.4 %copy-start.2 = (bf16[768,1536]{1,0:T(8,128)(2,1)S(1)}, bf16[768,1536]{1,0:T(8,128)(2,1)}, u32[]{:S(2)}) copy-start(bf16[768,1536]{1,0:T(8,128)(2,1)} %param.16) | copy-start | bytes 7077892
  2200.7 134.4 %copy-start.28 = (f32[1536]{0:T(1024)S(1)}, f32[1536]{0:T(1024)}, u32[]{:S(2)}) copy-start(f32[1536]{0:T(1024)} %copy-done.27) | copy-start | bytes 18436
  2200.7 134.4 %copy-start.34 = (f32[768]{0:T(1024)S(1)}, f32[768]{0:T(1024)}, u32[]{:S(2)}) copy-start(f32[768]{0:T(1024)} %copy-done.33) | copy-start | bytes 9220
  2201.5 136.8 %copy-start.37 = (f32[1536]{0:T(1024)S(1)}, f32[1536]{0:T(1024)}, u32[]{:S(2)}) copy-start(f32[1536]{0:T(1024)} %get-tuple-element.294) | copy-start | bytes 18436
  2201.5 231.8 %copy-start.26 = (f32[1536]{0:T(1024)S(1)}, f32[1536]{0:T(1024)}, u32[]{:S(2)}) copy-start(f32[1536]{0:T(1024)} %copy-done.25) | copy-start | bytes 18436
  2201.5 231.8 %copy-start.30 = (f32[768]{0:T(1024)S(1)}, f32[768]{0:T(1024)}, u32[]{:S(2)}) copy-start(f32[768]{0:T(1024)} %copy-done.29) | copy-start | bytes 9220
  2201.6 231.8 %copy-start.36 = (f32[768]{0:T(1024)S(1)}, f32[768]{0:T(1024)}, u32[]{:S(2)}) copy-start(f32[768]{0:T(1024)} %copy-done.35) | copy-start | bytes 9220
  (37 other events, 902.2 us)
Sparse Core Ops, SparseCore 0:
  36.6 94.4 all-gather.9
  132.7 22.7 all-gather.11
  157.1 22.4 all-gather.13
  443.9 170.5 reduce-scatter.11
  616.0 38.1 all-gather.19
  656.5 95.1 all-gather.15
  753.3 38.2 all-gather.17
  793.2 37.1 all-gather.21
  832.2 95.0 all-gather.23
  990.7 170.7 reduce-scatter.15
  1172.2 96.1 all-gather.25
  1270.6 40.3 reduce-scatter.31
  1313.3 39.6 reduce-scatter.29
  1355.2 39.6 reduce-scatter.27
  2107.9 31.9 reduce-scatter.21
  2142.0 30.1 reduce-scatter.23
  2174.4 31.2 reduce-scatter.25
  2207.8 31.1 reduce-scatter.19
  2242.1 92.9 reduce-scatter.17
  2338.1 95.1 reduce-scatter.13
where the time goes:
time: 2460 us; the launch traced here: 2450 us
  matrix products  1070 us (43%)
  waiting for transfers between devices  926 us (38%)
  other arithmetic  165 us (7%)
  local copies, waits for them, and re-layouts  148 us (6%)
  blocking collectives  80.7 us (3%)
  loops' own time  36.3 us (1%)
    dot_general x6, matrix products, backward_block(): jnp.einsum('cgqk,qcgd->kcd', grad_raw, query_block, preferred_element_typ...  225 us
    dot_general x6, matrix products, backward_block(): jnp.einsum('cgqk,kcd->qcgd', grad_raw, key_rot, preferred_element_type=jn...  211 us
    reduce_scatter x1, waiting for transfers between devices, on_device(): lax.psum_scatter(dot_cols(grad_gate_lin, gate_weight) + dot_cols(grad_up_...  171 us
    reduce_scatter x1, waiting for transfers between devices, on_device(): lax.psum_scatter(matrix_product(attn_out, out_weight), 'tensor', scatter_...  170 us
    dot_general x12, matrix products, block_scores(): jnp.einsum('qcgd,kcd->cgqk', query_block, key_rot, preferred_element_type...  141 us
    dot_general x7, matrix products, dot_cols(): lax.dot_general(left, right, (((1,), (1,)), ((), ())), preferred_element_...  114 us
    dynamic_update_slice x12, local copies, waits for them, and re-layouts, on_device(): lax.scan(backward_block, (zero_keys, zero_keys), begins)  112 us
    all_gather x1, waiting for transfers between devices, on_device(): ffn_rows = lax.all_gather(ffn_input, 'tensor', axis=0, tiled=True)  97.4 us
  transfers between devices with their start and end apart: 20, of which 13 were waited for; matrix products, arithmetic and copies ran while one was open for 52% of the time, Pallas kernels for 0%

commit v1 on v0

--- a/solution.py
+++ b/solution.py
@@ -1,6 +1,9 @@
+import functools
 import jax
 import jax.numpy as jnp
 from jax import lax
+from jax.experimental import pallas as pl
+from jax.experimental.pallas import tpu as pltpu
 from jax.sharding import PartitionSpec as P
 
 QUERY_HEADS = 16
@@ -79,6 +82,310 @@
 def norm_back(grad_normed, normed, inverse, gain):
     scaled = grad_normed * gain
     return inverse * (scaled - normed * jnp.mean(scaled * normed, axis=-1, keepdims=True))
+
+
+LOG2E = 1.4426950408889634
+
+
+def dot_f32(left, right):
+    return jnp.dot(left, right, preferred_element_type=jnp.float32)
+
+
+def block_mask(kv_block, q_block, block, starts, diagonal):
+    keys = kv_block * block + lax.broadcasted_iota(jnp.int32, (block, starts.shape[1]), 0)
+    allowed = keys >= starts
+    if diagonal:
+        group = starts.shape[1] // block
+        lanes = lax.broadcasted_iota(jnp.int32, (1, block), 1) + q_block * block
+        allowed = allowed & (keys <= jnp.concatenate([lanes] * group, axis=1))
+    return allowed
+
+
+def forward_kernel(
+    low_ref, high_ref, start_ref, qkv_ref, out_ref, lse_ref, qt_ref, k_ref, vt_ref, acc_ref,
+    *, heads, kv_heads, block, scale,
+):
+    step = pl.program_id(0)
+    rows = qkv_ref.shape[0]
+    group = heads // kv_heads
+    factor = scale * LOG2E
+    q_width = heads * HEAD_SIZE
+    k_width = kv_heads * HEAD_SIZE
+
+    @pl.when(step == 0)
+    def _():
+        @pl.loop(0, rows // block)
+        def _(at):
+            here = pl.ds(pl.multiple_of(at * block, block), block)
+            turned = qkv_ref[here, :].T
+            qt_ref[:, here] = turned[:q_width]
+            for kv in range(kv_heads):
+                begin = q_width + kv * HEAD_SIZE
+                k_ref[kv, here, :] = turned[begin : begin + HEAD_SIZE].T
+                begin = begin + k_width
+                vt_ref[kv, :HEAD_SIZE, here] = turned[begin : begin + HEAD_SIZE]
+                vt_ref[kv, HEAD_SIZE:, here] = jnp.ones((16, block), jnp.bfloat16)
+
+    here = pl.ds(pl.multiple_of(step * block, block), block)
+    starts = jnp.concatenate([start_ref[:, here]] * group, axis=1)
+    turned_queries = [
+        jnp.concatenate(
+            [
+                qt_ref[(kv * group + g) * HEAD_SIZE : (kv * group + g + 1) * HEAD_SIZE, here]
+                for g in range(group)
+            ],
+            axis=1,
+        )
+        for kv in range(kv_heads)
+    ]
+
+    def scores(kv, kv_block, masked, diagonal):
+        there = pl.ds(pl.multiple_of(kv_block * block, block), block)
+        raw = dot_f32(k_ref[kv, there, :], turned_queries[kv])
+        if masked:
+            raw = jnp.where(
+                block_mask(kv_block, step, block, starts, diagonal), raw, masked_value
+            )
+        return raw
+
+    def attend(kv, kv_block, probs):
+        there = pl.ds(pl.multiple_of(kv_block * block, block), block)
+        return dot_f32(vt_ref[kv, :, there], probs.astype(jnp.bfloat16))
+
+    largest = []
+    for kv in range(kv_heads):
+        raw = scores(kv, step, True, True)
+        top = jnp.max(raw, axis=0, keepdims=True)
+        acc_ref[kv] = attend(kv, step, jnp.exp2((raw - top) * factor))
+        largest.append(top)
+
+    def more(masked):
+        def body(kv_block, tops):
+            result = []
+            for kv in range(kv_heads):
+                raw = scores(kv, kv_block, masked, False)
+                top = jnp.maximum(tops[kv], jnp.max(raw, axis=0, keepdims=True))
+                shrink = jnp.exp2((tops[kv] - top) * factor)
+                acc_ref[kv] = acc_ref[kv] * shrink + attend(
+                    kv, kv_block, jnp.exp2((raw - top) * factor)
+                )
+                result.append(top)
+            return tuple(result)
+
+        return body
+
+    low = low_ref[step]
+    high = jnp.minimum(high_ref[step], step)
+    tops = lax.fori_loop(low, high, more(True), tuple(largest))
+    tops = lax.fori_loop(jnp.maximum(low, high), step, more(False), tops)
+    outs = []
+    for kv in range(kv_heads):
+        total = acc_ref[kv, HEAD_SIZE : HEAD_SIZE + 1, :]
+        result = (acc_ref[kv, :HEAD_SIZE, :] / total).astype(jnp.bfloat16)
+        logs = tops[kv] * factor + jnp.log2(total)
+        for g in range(group):
+            outs.append(result[:, g * block : (g + 1) * block])
+            lse_ref[kv * group + g : kv * group + g + 1, :] = logs[:, g * block : (g + 1) * block]
+    out_ref[...] = jnp.concatenate(outs, axis=0).T
+
+
+def attention_forward(qkv, starts, low, high, heads, kv_heads, block):
+    rows, width = qkv.shape
+    q_width = heads * HEAD_SIZE
+    group = heads // kv_heads
+    return pl.pallas_call(
+        functools.partial(
+            forward_kernel, heads=heads, kv_heads=kv_heads, block=block, scale=HEAD_SIZE**-0.5
+        ),
+        grid_spec=pltpu.PrefetchScalarGridSpec(
+            num_scalar_prefetch=2,
+            grid=(rows // block,),
+            in_specs=[
+                pl.BlockSpec((1, rows), lambda i, *_: (0, 0)),
+                pl.BlockSpec((rows, width), lambda i, *_: (0, 0)),
+            ],
+            out_specs=[
+                pl.BlockSpec((block, q_width), lambda i, *_: (i, 0)),
+                pl.BlockSpec((heads, block), lambda i, *_: (0, i)),
+            ],
+            scratch_shapes=[
+                pltpu.VMEM((q_width, rows), jnp.bfloat16),
+                pltpu.VMEM((kv_heads, rows, HEAD_SIZE), jnp.bfloat16),
+                pltpu.VMEM((kv_heads, HEAD_SIZE + 16, rows), jnp.bfloat16),
+                pltpu.VMEM((kv_heads, HEAD_SIZE + 16, group * block), jnp.float32),
+            ],
+        ),
+        out_shape=[
+            jax.ShapeDtypeStruct((rows, q_width), jnp.bfloat16),
+            jax.ShapeDtypeStruct((heads, rows), jnp.float32),
+        ],
+        name="attention_forward",
+    )(low, high, starts, qkv)
+
+
+def unrotate_turned(values, cosine, sine_table):
+    half = HEAD_SIZE // 2
+    front, back = values[:half], values[half:]
+    return jnp.concatenate(
+        [front * cosine + back * sine_table, back * cosine - front * sine_table], axis=0
+    )
+
+
+def backward_kernel(
+    low_ref, high_ref, start_ref, qkv_ref, out_ref, grad_ref, lse_ref, cos_ref, sin_ref,
+    result_ref, k_ref, kt_ref, v_ref, dk_ref, dv_ref, dq_ref, turned_ref,
+    *, heads, kv_heads, block, scale,
+):
+    step = pl.program_id(0)
+    rows = qkv_ref.shape[0]
+    group = heads // kv_heads
+    factor = scale * LOG2E
+    q_width = heads * HEAD_SIZE
+    k_width = kv_heads * HEAD_SIZE
+
+    @pl.when(step == 0)
+    def _():
+        dk_ref[...] = jnp.zeros_like(dk_ref)
+        dv_ref[...] = jnp.zeros_like(dv_ref)
+
+        @pl.loop(0, rows // block)
+        def _(at):
+            here = pl.ds(pl.multiple_of(at * block, block), block)
+            turned = qkv_ref[here, :].T
+            for kv in range(kv_heads):
+                begin = q_width + kv * HEAD_SIZE
+                kt_ref[kv, :, here] = turned[begin : begin + HEAD_SIZE]
+                k_ref[kv, here, :] = turned[begin : begin + HEAD_SIZE].T
+                begin = begin + k_width
+                v_ref[kv, here, :] = turned[begin : begin + HEAD_SIZE].T
+
+    here = pl.ds(pl.multiple_of(step * block, block), block)
+    starts = jnp.concatenate([start_ref[:, here]] * group, axis=1)
+    turned_q = qkv_ref[here, :].T
+    turned_grad = grad_ref[...].T
+    turned_out = out_ref[...].T
+    product = turned_grad.astype(jnp.float32) * turned_out.astype(jnp.float32)
+    queries, queries_turned, grads, grads_turned, inners, logs = [], [], [], [], [], []
+    for kv in range(kv_heads):
+        pieces = [
+            (slice((kv * group + g) * HEAD_SIZE, (kv * group + g + 1) * HEAD_SIZE))
+            for g in range(group)
+        ]
+        queries_turned.append(jnp.concatenate([turned_q[s] for s in pieces], axis=1))
+        grads_turned.append(jnp.concatenate([turned_grad[s] for s in pieces], axis=1))
+        queries.append(jnp.concatenate([turned_q[s].T for s in pieces], axis=0))
+        grads.append(jnp.concatenate([turned_grad[s].T for s in pieces], axis=0))
+        inners.append(
+            jnp.concatenate([jnp.sum(product[s], axis=0, keepdims=True) for s in pieces], axis=1)
+        )
+        logs.append(
+            jnp.concatenate(
+                [lse_ref[kv * group + g : kv * group + g + 1, :] for g in range(group)], axis=1
+            )
+        )
+
+    def block_step(kv_block, masked, diagonal):
+        there = pl.ds(pl.multiple_of(kv_block * block, block), block)
+        if masked:
+            allowed = block_mask(kv_block, step, block, starts, diagonal)
+        for kv in range(kv_heads):
+            raw = dot_f32(k_ref[kv, there, :], queries_turned[kv])
+            if masked:
+                raw = jnp.where(allowed, raw, masked_value)
+            probs = jnp.exp2(raw * factor - logs[kv])
+            grad_soft = dot_f32(v_ref[kv, there, :], grads_turned[kv])
+            grad_raw = (probs * (grad_soft - inners[kv])).astype(jnp.bfloat16)
+            dv_ref[kv, there, :] += dot_f32(probs.astype(jnp.bfloat16), grads[kv])
+            dk_ref[kv, there, :] += dot_f32(grad_raw, queries[kv])
+            dq = dot_f32(kt_ref[kv, :, there], grad_raw)
+            if diagonal:
+                dq_ref[kv] = dq
+            else:
+                dq_ref[kv] += dq
+
+    block_step(step, True, True)
+    low = low_ref[step]
+    high = jnp.minimum(high_ref[step], step)
+
+    @pl.loop(low, high)
+    def _(kv_block):
+        block_step(kv_block, True, False)
+
+    @pl.loop(jnp.maximum(low, high), step)
+    def _(kv_block):
+        block_step(kv_block, False, False)
+
+    cosine, sine_table = cos_ref[:, here], sin_ref[:, here]
+    for kv in range(kv_heads):
+        for g in range(group):
+            head = kv * group + g
+            turned = dq_ref[kv, :, g * block : (g + 1) * block] * scale
+            turned_ref[head * HEAD_SIZE : (head + 1) * HEAD_SIZE, here] = unrotate_turned(
+                turned, cosine, sine_table
+            ).astype(jnp.bfloat16)
+
+    @pl.when(step == pl.num_programs(0) - 1)
+    def _():
+        @pl.loop(0, rows // block)
+        def _(at):
+            here = pl.ds(pl.multiple_of(at * block, block), block)
+            pieces = [turned_ref[:, here]]
+            for kv in range(kv_heads):
+                turned = dk_ref[kv, here, :].T * scale
+                pieces.append(
+                    unrotate_turned(turned, cos_ref[:, here], sin_ref[:, here]).astype(
+                        jnp.bfloat16
+                    )
+                )
+            for kv in range(kv_heads):
+                pieces.append(dv_ref[kv, here, :].T.astype(jnp.bfloat16))
+            result_ref[here, :] = jnp.concatenate(pieces, axis=0).T
+
+
+def attention_backward(
+    qkv, out, grad, logs, starts, low, high, cosine, sine_table, heads, kv_heads, block
+):
+    rows, width = qkv.shape
+    q_width = heads * HEAD_SIZE
+    group = heads // kv_heads
+    half = HEAD_SIZE // 2
+    whole = lambda i, *_: (0, 0)
+    return pl.pallas_call(
+        functools.partial(
+            backward_kernel, heads=heads, kv_heads=kv_heads, block=block, scale=HEAD_SIZE**-0.5
+        ),
+        grid_spec=pltpu.PrefetchScalarGridSpec(
+            num_scalar_prefetch=2,
+            grid=(rows // block,),
+            in_specs=[
+                pl.BlockSpec((1, rows), whole),
+                pl.BlockSpec((rows, width), whole),
+                pl.BlockSpec((block, q_width), lambda i, *_: (i, 0)),
+                pl.BlockSpec((block, q_width), lambda i, *_: (i, 0)),
+                pl.BlockSpec((heads, block), lambda i, *_: (0, i)),
+                pl.BlockSpec((half, rows), whole),
+                pl.BlockSpec((half, rows), whole),
+            ],
+            out_specs=pl.BlockSpec((rows, width), whole),
+            scratch_shapes=[
+                pltpu.VMEM((kv_heads, rows, HEAD_SIZE), jnp.bfloat16),
+                pltpu.VMEM((kv_heads, HEAD_SIZE, rows), jnp.bfloat16),
+                pltpu.VMEM((kv_heads, rows, HEAD_SIZE), jnp.bfloat16),
+                pltpu.VMEM((kv_heads, rows, HEAD_SIZE), jnp.float32),
+                pltpu.VMEM((kv_heads, rows, HEAD_SIZE), jnp.float32),
+                pltpu.VMEM((kv_heads, HEAD_SIZE, group * block), jnp.float32),
+                pltpu.VMEM((q_width, rows), jnp.bfloat16),
+            ],
+        ),
+        out_shape=jax.ShapeDtypeStruct((rows, width), jnp.bfloat16),
+        name="attention_backward",
+    )(low, high, starts, qkv, out, grad, logs, cosine, sine_table)
+
+
+def block_bounds(starts, block):
+    firsts = starts[0, ::block]
+    lasts = starts[0, block - 1 :: block]
+    return firsts // block, (lasts + block - 1) // block
 
 
 def on_device(
@@ -116,7 +423,8 @@
     kv_local = key_weight.shape[1] // HEAD_SIZE
     group_width = QUERY_HEADS // KEY_VALUE_HEADS
     heads_local = kv_local * group_width
-    cosine, sine_table = angles_of(positions(segment_row))
+    position_ids = positions(segment_row)
+    cosine, sine_table = angles_of(position_ids)
     cosine_heads = cosine[:, None, None, :]
     sine_heads = sine_table[:, None, None, :]
     cosine_keys = cosine[:, None, :]
@@ -137,38 +445,20 @@
         .astype(jnp.bfloat16)
         .reshape(pack_rows, kv_local, HEAD_SIZE)
     )
-    rows_of_block = min(512, pack_rows)
-    block_list = pack_rows // rows_of_block
-    score_scale = HEAD_SIZE ** (-0.5)
-    key_index = jnp.arange(pack_rows, dtype=jnp.int32)
-    begins = jnp.arange(block_list, dtype=jnp.int32) * rows_of_block
-
-    def block_scores(begin_row):
-        query_block = lax.dynamic_slice_in_dim(query_rot, begin_row, rows_of_block, 0)
-        raw_scores = jnp.einsum(
-            "qcgd,kcd->cgqk", query_block, key_rot, preferred_element_type=jnp.float32
-        )
-        scores = raw_scores * score_scale
-        query_index = begin_row + jnp.arange(rows_of_block, dtype=jnp.int32)
-        query_segment = lax.dynamic_slice_in_dim(segment_row, begin_row, rows_of_block)
-        allowed = (query_segment[:, None] == segment_row[None, :]) & (
-            key_index[None, :] <= query_index[:, None]
-        )
-        return (query_block, jnp.where(allowed, scores, masked_value))
-
-    def forward_block(begin_row):
-        query_block, scores = block_scores(begin_row)
-        largest = jnp.max(scores, axis=-1, keepdims=True)
-        exp_scores = jnp.exp(scores - largest)
-        row_total = jnp.sum(exp_scores, axis=-1, keepdims=True)
-        softmax_rows = (exp_scores / row_total).astype(jnp.bfloat16)
-        attended = jnp.einsum(
-            "cgqk,kcd->qcgd", softmax_rows, rows_of_values, preferred_element_type=jnp.float32
-        )
-        return (attended.astype(jnp.bfloat16), largest[..., 0] + jnp.log(row_total[..., 0]))
-
-    attn_blocks, log_totals = lax.map(forward_block, begins)
-    attn_out = attn_blocks.reshape(pack_rows, heads_local * HEAD_SIZE)
+    qkv = jnp.concatenate(
+        [
+            query_rot.reshape(pack_rows, heads_local * HEAD_SIZE),
+            key_rot.reshape(pack_rows, kv_local * HEAD_SIZE),
+            rows_of_values.reshape(pack_rows, kv_local * HEAD_SIZE),
+        ],
+        axis=1,
+    )
+    starts = (jnp.arange(pack_rows, dtype=jnp.int32) - position_ids)[None, :]
+    low_512, high_512 = block_bounds(starts, 512)
+    low_256, high_256 = block_bounds(starts, 256)
+    attn_out, log_totals = attention_forward(
+        qkv, starts, low_512, high_512, heads_local, kv_local, 512
+    )
     branch = lax.psum_scatter(
         matrix_product(attn_out, out_weight), "tensor", scatter_dimension=0, tiled=True
     )
@@ -212,51 +502,26 @@
     grad_branch = grad_mid.astype(jnp.bfloat16)
     branch_rows = lax.all_gather(grad_branch, "tensor", axis=0, tiled=True)
     grad_out_w = dot_rows(attn_out, branch_rows)
-    grad_attended = (
-        dot_cols(branch_rows, out_weight)
-        .astype(jnp.bfloat16)
-        .reshape(pack_rows, kv_local, group_width, HEAD_SIZE)
-    )
-
-    def backward_block(running, begin_row):
-        key_grad, value_grad = running
-        query_block, scores = block_scores(begin_row)
-        log_block = lax.dynamic_index_in_dim(
-            log_totals, begin_row // rows_of_block, 0, keepdims=False
-        )
-        softmax_rows = jnp.exp(scores - log_block[..., None])
-        grad_block = lax.dynamic_slice_in_dim(grad_attended, begin_row, rows_of_block, 0)
-        grad_soft = jnp.einsum(
-            "qcgd,kcd->cgqk", grad_block, rows_of_values, preferred_element_type=jnp.float32
-        )
-        row_inner = jnp.sum(softmax_rows * grad_soft, axis=-1, keepdims=True)
-        grad_raw = (softmax_rows * (grad_soft - row_inner) * score_scale).astype(jnp.bfloat16)
-        query_grad = jnp.einsum(
-            "cgqk,kcd->qcgd", grad_raw, key_rot, preferred_element_type=jnp.float32
-        )
-        key_grad = key_grad + jnp.einsum(
-            "cgqk,qcgd->kcd", grad_raw, query_block, preferred_element_type=jnp.float32
-        )
-        value_grad = value_grad + jnp.einsum(
-            "cgqk,qcgd->kcd",
-            softmax_rows.astype(jnp.bfloat16),
-            grad_block,
-            preferred_element_type=jnp.float32,
-        )
-        return ((key_grad, value_grad), query_grad)
-
-    zero_keys = jnp.zeros((pack_rows, kv_local, HEAD_SIZE), jnp.float32)
-    (key_grad, value_grad), query_grads = lax.scan(backward_block, (zero_keys, zero_keys), begins)
-    query_grad = unrotate(
-        query_grads.reshape(pack_rows, kv_local, group_width, HEAD_SIZE), cosine_heads, sine_heads
-    )
-    query_grad = query_grad.astype(jnp.bfloat16).reshape(pack_rows, heads_local * HEAD_SIZE)
-    key_grad_low = (
-        unrotate(key_grad, cosine_keys, sine_keys)
-        .astype(jnp.bfloat16)
-        .reshape(pack_rows, kv_local * HEAD_SIZE)
-    )
-    value_grad_low = value_grad.astype(jnp.bfloat16).reshape(pack_rows, kv_local * HEAD_SIZE)
+    grad_attended = dot_cols(branch_rows, out_weight).astype(jnp.bfloat16)
+    grad_qkv = attention_backward(
+        qkv,
+        attn_out,
+        grad_attended,
+        log_totals,
+        starts,
+        low_256,
+        high_256,
+        cosine.T,
+        sine_table.T,
+        heads_local,
+        kv_local,
+        256,
+    )
+    query_grad, key_grad_low, value_grad_low = jnp.split(
+        grad_qkv,
+        [heads_local * HEAD_SIZE, (heads_local + kv_local) * HEAD_SIZE],
+        axis=1,
+    )
     grad_query_w = dot_rows(attn_rows, query_grad)
     grad_key_w = dot_rows(attn_rows, key_grad_low)
     grad_value_w = dot_rows(attn_rows, value_grad_low)

time: 2460 us -> 1540 us (0.63)
  matrix products: 1070 us -> 277 us
  local copies, waits for them, and re-layouts: 148 us -> 17.6 us
  other arithmetic: 165 us -> 65.3 us
  Pallas kernels: 0 us -> 91.7 us
  waiting for transfers between devices: 926 us -> 983 us
  loops' own time: 36.3 us -> 0 us
    dot_general x42 -> x0, matrix products: 802 us -> none  [the longest x6 225 us: backward_block(): jnp.einsum('cgqk,qcgd->kcd', grad_raw, query_block, preferred_element_typ...]
    dynamic_update_slice x12 -> x0, local copies, waits for them, and re-layouts: 112 us -> none  [on_device(): lax.scan(backward_block, (zero_keys, zero_keys), begins)]
    pallas_call x0 -> x2, Pallas kernels: none -> 91.7 us  [the longest x1 54.7 us: attention_backward(): pl.pallas_call(functools.partial(backward_kernel, heads=heads, kv_heads=k...]
    reduce_sum x6 -> x0, other arithmetic: 71.5 us -> none  [forward_block(): row_total = jnp.sum(exp_scores, axis=-1, keepdims=True)]
    another operation x2 -> x0, loops' own time: 36.3 us -> none  [the longest x1 24.1 us: on_device(): lax.scan(backward_block, (zero_keys, zero_keys), begins)]
    reduce_scatter x1, waiting for transfers between devices: 0.01 us -> 32.5 us  [on_device(): lax.psum_scatter(grad_out_w.astype(jnp.bfloat16), 'dp', scatter_dimension...]
    reduce_scatter x1, waiting for transfers between devices: 0.01 us -> 27.6 us  [on_device(): lax.psum_scatter(grad_value_w.astype(jnp.bfloat16), 'dp', scatter_dimensi...]
  transfers between devices with their start and end apart: 20 -> 20, of which waited for: 13 -> 15; matrix products, arithmetic and copies ran while one was open for 52% -> 17% of each run, Pallas kernels for 0% -> 6%
where the time goes in v1:
time: 1540 us; the launch traced here: 1530 us
  waiting for transfers between devices  983 us (64%)
  matrix products  277 us (18%)
  Pallas kernels  91.7 us (6%)
  blocking collectives  80.1 us (5%)
  other arithmetic  65.3 us (4%)
  local copies, waits for them, and re-layouts  17.6 us (1%)
  between operations  16.7 us (1%)
    reduce_scatter x1, waiting for transfers between devices, on_device(): lax.psum_scatter(dot_cols(grad_gate_lin, gate_weight) + dot_cols(grad_up_...  171 us
    reduce_scatter x1, waiting for transfers between devices, on_device(): lax.psum_scatter(matrix_product(attn_out, out_weight), 'tensor', scatter_...  170 us
    dot_general x7, matrix products, dot_cols(): lax.dot_general(left, right, (((1,), (1,)), ((), ())), preferred_element_...  111 us
    all_gather x1, waiting for transfers between devices, on_device(): cotangent_rows = lax.all_gather(cotangent, 'tensor', axis=0, tiled=True)  97 us
    all_gather x1, waiting for transfers between devices, on_device(): ffn_rows = lax.all_gather(ffn_input, 'tensor', axis=0, tiled=True)  96.8 us
    reduce_scatter x1, waiting for transfers between devices, on_device(): lax.psum_scatter((dot_cols(query_grad, query_weight) + dot_cols(key_grad_...  94.6 us
    dot_general x7, matrix products, matrix_product(): return jnp.dot(left, right, preferred_element_type=jnp.float32)  83.4 us
    dot_general x7, matrix products, dot_rows(): lax.dot_general(left, right, (((0,), (0,)), ((), ())), preferred_element_...  82.4 us
  transfers between devices with their start and end apart: 20, of which 15 were waited for; matrix products, arithmetic and copies ran while one was open for 17% of the time, Pallas kernels for 6%

profile of v1, /device:TPU:0, one launch (start us, length us, event | category | flops | bytes accessed | tf_op | source)
XLA Modules:
  0.0 1533.4 jit_solution(4155819026408578446)
XLA Ops:
  13.2 18.3 %all-reduce.6 = (bf16[1536]{0:T(1024)(128)(2,1)S(1)}, bf16[1536]{0:T(1024)(128)(2,1)S(1)}) all-reduce(bf16[1536]{0:T(1024)(128)(2,1)S(1)} %dynamic-update-slice, bf16[1536]{0:T(1024)(128)(2,1)S(1)} %dynamic-update-slice.1), channel_id=1, replica_groups=mesh['dp'=8,'tensor'=4] {'dp'}, use_global_device_ids=true, to_apply=%add | all-reduce | flops 3072 | bytes 12288
  38.0 15.7 %all_gather.42 = bf16[1536,192]{1,0:T(8,128)(2,1)S(1)} all-gather(bf16[192,192]{1,0:T(8,128)(2,1)S(1)} %copy-done.21), channel_id=1, replica_groups=mesh['dp'=8,'tensor'=4] {'dp'}, dimensions={0}, use_global_device_ids=true | all-gather | bytes 663552 | tf_op jit(solution)/shard_map/all_gather | solution.py:409
  53.7 16.4 %all_gather.43 = bf16[1536,192]{1,0:T(8,128)(2,1)S(1)} all-gather(bf16[192,192]{1,0:T(8,128)(2,1)S(1)} %copy-done.22), channel_id=1, replica_groups=mesh['dp'=8,'tensor'=4] {'dp'}, dimensions={0}, use_global_device_ids=true | all-gather | bytes 663552 | tf_op jit(solution)/shard_map/all_gather | solution.py:410
  72.8 57.6 %all-gather.10.cloned.1.call-done = bf16[3072,1536]{1,0:T(8,128)(2,1)} async-done(((bf16[768,1536]{1,0:T(8,128)(2,1)}), bf16[3072,1536]{1,0:T(8,128)(2,1)}) %all-gather.10.cloned.1.call-update) | async-done | bytes 9437200 | tf_op jit(solution)/shard_map/all_gather | solution.py:436
  138.6 16.3 %all-gather.12.cloned.1.call-done = bf16[1536,384]{1,0:T(8,128)(2,1)} async-done(((bf16[192,384]{1,0:T(8,128)(2,1)}), bf16[1536,384]{1,0:T(8,128)(2,1)}) %all-gather.12.cloned.1.call-update) | async-done | bytes 1179664 | tf_op jit(solution)/shard_map/all_gather | solution.py:408
  191.2 37.0 %attention_forward.1 = (bf16[3072,384]{1,0:T(8,128)(2,1)}, f32[4,3072]{1,0:T(4,128)}) custom-call(s32[6]{0:T(128)} %get-tuple-element.43.low_ref, s32[6]{0:T(128)} %get-tuple-element.42.high_ref, s32[1,3072]{1,0:T(1,128)} %copy-done.18, bf16[3072,768]{1,0:T(8,128)(2,1)} %pad_maximum_fusion.qkv_ref), custom_call_target="tpu_custom_call" | custom-call | tf_op jit(solution)/shard_map/attention_forward/pallas_call | solution.py:196
  240.0 170.0 %reduce-scatter.12.cloned.1.call-done = f32[768,1536]{1,0:T(8,128)} async-done(((f32[3072,1536]{1,0:T(8,128)}), f32[768,1536]{1,0:T(8,128)}) %reduce-scatter.12.cloned.1.call-update) | async-done | bytes 4718608 | tf_op jit(solution)/shard_map/reduce_scatter | solution.py:462
  419.3 30.4 %all-gather.20.cloned.1.call-done = bf16[1536,1024]{1,0:T(8,128)(2,1)} async-done(((bf16[192,1024]{1,0:T(8,128)(2,1)}), bf16[1536,1024]{1,0:T(8,128)(2,1)}) %all-gather.20.cloned.1.call-update) | async-done | bytes 3145744 | tf_op jit(solution)/shard_map/all_gather | solution.py:413
  449.7 96.8 %all-gather.16.cloned.1.call-done = bf16[3072,1536]{1,0:T(8,128)(2,1)} async-done(((bf16[768,1536]{1,0:T(8,128)(2,1)}), bf16[3072,1536]{1,0:T(8,128)(2,1)}) %all-gather.16.cloned.1.call-update) | async-done | bytes 9437200 | tf_op jit(solution)/shard_map/all_gather | solution.py:470
  546.5 16.3 %fusion.26 = f32[3072,1024]{1,0:T(8,128)} fusion(bf16[3072,1536]{1,0:T(8,128)(2,1)} %all-gather.16.cloned.1.call-done, bf16[1536,1024]{1,0:T(8,128)(2,1)} %all-gather.20.cloned.1.call-done), kind=kOutput, calls=%fused_computation.96 | convolution fusion | flops 9663676416 | bytes 25165824 | tf_op jit(solution)/shard_map/dot_general | solution.py:21
  562.8 23.6 %all-gather.18.cloned.1.call-done = bf16[1536,1024]{1,0:T(8,128)(2,1)} async-done(((bf16[192,1024]{1,0:T(8,128)(2,1)}), bf16[1536,1024]{1,0:T(8,128)(2,1)}) %all-gather.18.cloned.1.call-update) | async-done | bytes 3145744 | tf_op jit(solution)/shard_map/all_gather | solution.py:412
  586.4 16.1 %fusion.25 = f32[3072,1024]{1,0:T(8,128)} fusion(bf16[3072,1536]{1,0:T(8,128)(2,1)} %all-gather.16.cloned.1.call-done, bf16[1536,1024]{1,0:T(8,128)(2,1)} %all-gather.18.cloned.1.call-done), kind=kOutput, calls=%fused_computation.95 | convolution fusion | flops 9663676416 | bytes 25165824 | tf_op jit(solution)/shard_map/dot_general | solution.py:21
  602.5 22.7 %all-gather.22.cloned.1.call-done = bf16[1024,1536]{0,1:T(8,128)(2,1)} async-done(((bf16[1024,192]{0,1:T(8,128)(2,1)}), bf16[1024,1536]{0,1:T(8,128)(2,1)}) %all-gather.22.cloned.1.call-update) | async-done | bytes 3145744 | tf_op jit(solution)/shard_map/all_gather | solution.py:414
  625.2 97.0 %all-gather.24.cloned.1.call-done = bf16[3072,1536]{1,0:T(8,128)(2,1)} async-done(((bf16[768,1536]{1,0:T(8,128)(2,1)}), bf16[3072,1536]{1,0:T(8,128)(2,1)}) %all-gather.24.cloned.1.call-update) | async-done | bytes 9437200 | tf_op jit(solution)/shard_map/all_gather | solution.py:485
  722.2 24.1 %multiply_convert_fusion = (bf16[3072,1024]{1,0:T(8,128)(2,1)}, bf16[3072,1024]{1,0:T(8,128)(2,1)S(1)}, bf16[3072,1024]{1,0:T(8,128)(2,1)}) fusion(f32[3072,1024]{1,0:T(8,128)} %fusion.25, f32[3072,1024]{1,0:T(8,128)} %fusion.26, bf16[3072,1536]{1,0:T(8,128)(2,1)} %all-gather.24.cloned.1.call-done, bf16[1024,1536]{0,1:T(8,128)(2,1)} %all-gather.22.cloned.1.call-done), kind=kOutput, calls=%fused_computation.2 | convolution fusion | flops 9710862336 | bytes 56623104 | tf_op jit(solution)/shard_map/dot_general | solution.py:31
  746.3 17.8 %fusion.27 = f32[3072,1536]{1,0:T(8,128)} fusion(bf16[3072,1024]{1,0:T(8,128)(2,1)S(1)} %get-tuple-element.28, bf16[1536,1024]{1,0:T(8,128)(2,1)} %all-gather.18.cloned.1.call-done), kind=kOutput, calls=%fused_computation.97 | convolution fusion | flops 9663676416 | bytes 28311552 | tf_op jit(solution)/shard_map/dot_general | solution.py:31
  764.1 20.8 %convolution_add_fusion = f32[3072,1536]{1,0:T(8,128)} fusion(f32[3072,1536]{1,0:T(8,128)} %fusion.27, bf16[3072,1024]{1,0:T(8,128)(2,1)} %get-tuple-element.27, bf16[1536,1024]{1,0:T(8,128)(2,1)S(1)} %copy-done.32), kind=kOutput, calls=%fused_computation.1 | convolution fusion | flops 9668395008 | bytes 47185920 | tf_op jit(solution)/shard_map/dot_general | solution.py:31
  785.0 170.8 %reduce-scatter.16.cloned.1.call-done = f32[768,1536]{1,0:T(8,128)} async-done(((f32[3072,1536]{1,0:T(8,128)}), f32[768,1536]{1,0:T(8,128)}) %reduce-scatter.16.cloned.1.call-update) | async-done | bytes 4718608 | tf_op jit(solution)/shard_map/reduce_scatter | solution.py:494
  966.5 16.0 %convolution_convert_fusion.2 = bf16[1024,1536]{0,1:T(8,128)(2,1)} fusion(bf16[3072,1024]{1,0:T(8,128)(2,1)} %get-tuple-element.29, bf16[3072,1536]{1,0:T(8,128)(2,1)} %all-gather.24.cloned.1.call-done), kind=kOutput, calls=%fused_computation.31 | convolution fusion | flops 9665249280 | bytes 18874368 | tf_op jit(solution)/shard_map/dot_general | solution.py:25
  982.6 15.6 %convolution_convert_fusion.3 = bf16[1536,1024]{1,0:T(8,128)(2,1)} fusion(bf16[3072,1536]{1,0:T(8,128)(2,1)} %all-gather.16.cloned.1.call-done, bf16[3072,1024]{1,0:T(8,128)(2,1)} %get-tuple-element.27), kind=kOutput, calls=%fused_computation.32 | convolution fusion | flops 9665249280 | bytes 18874368 | tf_op jit(solution)/shard_map/dot_general | solution.py:25
  998.3 15.9 %convolution_convert_fusion.4 = bf16[1536,1024]{1,0:T(8,128)(2,1)} fusion(bf16[3072,1536]{1,0:T(8,128)(2,1)} %all-gather.16.cloned.1.call-done, bf16[3072,1024]{1,0:T(8,128)(2,1)} %copy-done.33), kind=kOutput, calls=%fused_computation.33 | convolution fusion | flops 9665249280 | bytes 18874368 | tf_op jit(solution)/shard_map/dot_general | solution.py:25
  1019.7 43.1 %all-gather.26.cloned.1.call-done = bf16[3072,1536]{1,0:T(8,128)(2,1)} async-done(((bf16[768,1536]{1,0:T(8,128)(2,1)}), bf16[3072,1536]{1,0:T(8,128)(2,1)}) %all-gather.26.cloned.1.call-update) | async-done | bytes 9437200 | tf_op jit(solution)/shard_map/all_gather | solution.py:503
  1072.7 54.7 %attention_backward.1 = bf16[3072,768]{1,0:T(8,128)(2,1)} custom-call(s32[12]{0:T(128)} %get-tuple-element.45.low_ref, s32[12]{0:T(128)} %get-tuple-element.44.high_ref, s32[1,3072]{1,0:T(1,128)} %copy-done.18, bf16[3072,768]{1,0:T(8,128)(2,1)} %pad_maximum_fusion.qkv_ref, bf16[3072,384]{1,0:T(8,128)(2,1)} %get-tuple-element.13.out_ref, ...), custom_call_target="tpu_custom_call" | custom-call | tf_op jit(solution)/shard_map/attention_backward/pallas_call | solution.py:353
  1183.9 18.1 %add_convert_fusion = bf16[3072,1536]{1,0:T(8,128)(2,1)} fusion(f32[3072,1536]{1,0:T(8,128)} %fusion.13, f32[3072,1536]{1,0:T(8,128)} %fusion.18, bf16[1536,192]{1,0:T(8,128)(2,1)S(1)} %copy-done.9, bf16[3072,768]{1,0:T(8,128)(2,1)} %attention_backward.1), kind=kOutput, calls=%fused_computation | convolution fusion | flops 1826095104 | bytes 49348608 | tf_op jit(solution)/shard_map/dot_general | solution.py:31
  1203.9 14.9 convolution_convert_fusion
  1227.2 27.6 %reduce-scatter.24.cloned.1.call-done = bf16[192,192]{1,0:T(8,128)(2,1)} async-done(((bf16[1536,192]{1,0:T(8,128)(2,1)}), bf16[192,192]{1,0:T(8,128)(2,1)}) %reduce-scatter.24.cloned.1.call-update) | async-done | bytes 73744 | tf_op jit(solution)/shard_map/reduce_scatter | solution.py:554
  1256.4 32.5 %reduce-scatter.26.cloned.1.call-done = bf16[384,192]{0,1:T(8,128)(2,1)} async-done(((bf16[384,1536]{0,1:T(8,128)(2,1)}), bf16[384,192]{0,1:T(8,128)(2,1)}) %reduce-scatter.26.cloned.1.call-update) | async-done | bytes 147472 | tf_op jit(solution)/shard_map/reduce_scatter | solution.py:557
  1290.6 32.2 %reduce-scatter.20.cloned.1.call-done = bf16[192,384]{1,0:T(8,128)(2,1)} async-done(((bf16[1536,384]{1,0:T(8,128)(2,1)}), bf16[192,384]{1,0:T(8,128)(2,1)}) %reduce-scatter.20.cloned.1.call-update) | async-done | bytes 147472 | tf_op jit(solution)/shard_map/reduce_scatter | solution.py:548
  1324.4 94.6 %reduce-scatter.18.cloned.1.call-done = bf16[768,1536]{1,0:T(8,128)(2,1)} async-done(((bf16[3072,1536]{1,0:T(8,128)(2,1)}), bf16[768,1536]{1,0:T(8,128)(2,1)}) %reduce-scatter.18.cloned.1.call-update) | async-done | bytes 2359312 | tf_op jit(solution)/shard_map/reduce_scatter | solution.py:528
  1422.2 15.7 %all-reduce.4 = (bf16[1536]{0:T(1024)(128)(2,1)S(1)}, bf16[1536]{0:T(1024)(128)(2,1)S(1)}) all-reduce(f32[1536]{0:T(1024)S(1)} %get-tuple-element.17, f32[1536]{0:T(1024)S(1)} %copy-done.28), channel_id=1, replica_groups=mesh['dp'=8,'tensor'=4] {'tensor'}, use_global_device_ids=true, to_apply=%region_11.12 | all-reduce | flops 3072 | bytes 18432 | tf_op jit(solution)/shard_map/psum | solution.py:540
  1437.9 13.9 all-reduce.5
  1453.1 64.1 %reduce-scatter.14.cloned.1.call-done = bf16[768,1536]{1,0:T(8,128)(2,1)} async-done(((bf16[3072,1536]{1,0:T(8,128)(2,1)}), bf16[768,1536]{1,0:T(8,128)(2,1)}) %reduce-scatter.14.cloned.1.call-update) | async-done | bytes 2359312 | tf_op jit(solution)/shard_map/reduce_scatter | solution.py:478
  (173 shorter events, 190.0 us)
Async XLA Ops:
  7.2 123.3 %all-gather.10.cloned.1.call-start = ((), (), s32[]{:S(2)}) async-start(), calls=%async_computation.11 | async-start | bytes 11796480 | tf_op jit(solution)/shard_map/all_gather | solution.py:436
  35.9 119.0 %all-gather.12.cloned.1.call-start = ((), (), s32[]{:S(2)}) async-start(), calls=%async_computation.12 | async-start | bytes 1327104 | tf_op jit(solution)/shard_map/all_gather | solution.py:408
  36.6 191.5 %all-gather.14.cloned.1.call-start = ((), (), s32[]{:S(2)}) async-start(), calls=%async_computation.13 | async-start | bytes 1327104 | tf_op jit(solution)/shard_map/all_gather | solution.py:411
  37.4 372.6 %reduce-scatter.12.cloned.1.call-start = ((), (), s32[]{:S(2)}) async-start(), calls=%async_computation.14 | async-start | bytes 23592960 | tf_op jit(solution)/shard_map/reduce_scatter | solution.py:462
  37.4 99.9 %copy-start.29 = (f32[48]{0:T(128)}, f32[48]{0:T(128)S(1)}, u32[]{:S(2)}) copy-start(f32[48]{0:T(128)S(1)} %multiply_power_fusion) | copy-start | bytes 580
  239.3 170.7 %copy-start.1 = (bf16[768,1536]{1,0:T(8,128)(2,1)S(1)}, bf16[768,1536]{1,0:T(8,128)(2,1)}, u32[]{:S(2)}) copy-start(bf16[768,1536]{1,0:T(8,128)(2,1)} %param.12) | copy-start | bytes 7077892
  239.3 210.4 %all-gather.20.cloned.1.call-start = ((), (), s32[]{:S(2)}) async-start(), calls=%async_computation.17 | async-start | bytes 3538944 | tf_op jit(solution)/shard_map/all_gather | solution.py:413
  239.9 306.6 %all-gather.16.cloned.1.call-start = ((), (), s32[]{:S(2)}) async-start(), calls=%async_computation.15 | async-start | bytes 11796480 | tf_op jit(solution)/shard_map/all_gather | solution.py:470
  240.0 721.5 %copy-start.12 = (f32[1536]{0:T(1024)}, f32[1536]{0:T(1024)S(1)}, u32[]{:S(2)}) copy-start(f32[1536]{0:T(1024)S(1)} %convert_element_type.134) | copy-start | bytes 18436
  413.0 548.5 %copy-start.19 = (f32[768]{0:T(1024)}, f32[768]{0:T(1024)S(1)}, u32[]{:S(2)}) copy-start(f32[768]{0:T(1024)S(1)} %add_rsqrt_fusion) | copy-start | bytes 9220
  417.0 169.4 %all-gather.18.cloned.1.call-start = ((), (), s32[]{:S(2)}) async-start(), calls=%async_computation.16 | async-start | bytes 3538944 | tf_op jit(solution)/shard_map/all_gather | solution.py:412
  417.8 207.4 %all-gather.22.cloned.1.call-start = ((), (), s32[]{:S(2)}) async-start(), calls=%async_computation.18 | async-start | bytes 3538944 | tf_op jit(solution)/shard_map/all_gather | solution.py:414
  418.5 303.7 %all-gather.24.cloned.1.call-start = ((), (), s32[]{:S(2)}) async-start(), calls=%async_computation.20 | async-start | bytes 11796480 | tf_op jit(solution)/shard_map/all_gather | solution.py:485
  419.2 536.6 %reduce-scatter.16.cloned.1.call-start = ((), (), s32[]{:S(2)}) async-start(), calls=%async_computation.21 | async-start | bytes 23592960 | tf_op jit(solution)/shard_map/reduce_scatter | solution.py:494
  784.9 177.2 %copy-start.4 = (bf16[768,1536]{1,0:T(8,128)(2,1)S(1)}, bf16[768,1536]{1,0:T(8,128)(2,1)}, u32[]{:S(2)}) copy-start(bf16[768,1536]{1,0:T(8,128)(2,1)} %param.13) | copy-start | bytes 7077892
  784.9 277.8 %all-gather.26.cloned.1.call-start = ((), (), s32[]{:S(2)}) async-start(), calls=%async_computation.22 | async-start | bytes 11796480 | tf_op jit(solution)/shard_map/all_gather | solution.py:503
  966.4 253.3 %reduce-scatter.32.cloned.1.call-start = ((), (), s32[]{:S(2)}) async-start(), calls=%async_computation.30 | async-start | bytes 3538944 | tf_op jit(solution)/shard_map/reduce_scatter | solution.py:566
  982.5 239.2 %reduce-scatter.30.cloned.1.call-start = ((), (), s32[]{:S(2)}) async-start(), calls=%async_computation.29 | async-start | bytes 3538944 | tf_op jit(solution)/shard_map/reduce_scatter | solution.py:563
  998.3 225.4 %reduce-scatter.28.cloned.1.call-start = ((), (), s32[]{:S(2)}) async-start(), calls=%async_computation.28 | async-start | bytes 3538944 | tf_op jit(solution)/shard_map/reduce_scatter | solution.py:560
  1014.2 211.4 %reduce-scatter.22.cloned.1.call-start = ((), (), s32[]{:S(2)}) async-start(), calls=%async_computation.25 | async-start | bytes 884736 | tf_op jit(solution)/shard_map/reduce_scatter | solution.py:551
  1135.2 119.6 %reduce-scatter.24.cloned.1.call-start = ((), (), s32[]{:S(2)}) async-start(), calls=%async_computation.26 | async-start | bytes 884736 | tf_op jit(solution)/shard_map/reduce_scatter | solution.py:554
  1144.2 144.7 %reduce-scatter.26.cloned.1.call-start = ((), (), s32[]{:S(2)}) async-start(), calls=%async_computation.27 | async-start | bytes 1327104 | tf_op jit(solution)/shard_map/reduce_scatter | solution.py:557
  1153.1 169.6 %reduce-scatter.20.cloned.1.call-start = ((), (), s32[]{:S(2)}) async-start(), calls=%async_computation.24 | async-start | bytes 1327104 | tf_op jit(solution)/shard_map/reduce_scatter | solution.py:548
  1162.8 256.2 %reduce-scatter.18.cloned.1.call-start = ((), (), s32[]{:S(2)}) async-start(), calls=%async_computation.23 | async-start | bytes 11796480 | tf_op jit(solution)/shard_map/reduce_scatter | solution.py:528
  1202.0 315.1 %reduce-scatter.14.cloned.1.call-start = ((), (), s32[]{:S(2)}) async-start(), calls=%async_computation.19 | async-start | bytes 11796480 | tf_op jit(solution)/shard_map/reduce_scatter | solution.py:478
  1218.9 200.1 %copy-start.2 = (bf16[768,1536]{1,0:T(8,128)(2,1)S(1)}, bf16[768,1536]{1,0:T(8,128)(2,1)}, u32[]{:S(2)}) copy-start(bf16[768,1536]{1,0:T(8,128)(2,1)} %param.12) | copy-start | bytes 7077892
  1218.9 200.1 %copy-start.15 = (f32[1536]{0:T(1024)S(1)}, f32[1536]{0:T(1024)}, u32[]{:S(2)}) copy-start(f32[1536]{0:T(1024)} %copy-done.14) | copy-start | bytes 18436
  1218.9 200.1 %copy-start.24 = (f32[768]{0:T(1024)S(1)}, f32[768]{0:T(1024)}, u32[]{:S(2)}) copy-start(f32[768]{0:T(1024)} %copy-done.23) | copy-start | bytes 9220
  1219.7 202.5 %copy-start.28 = (f32[1536]{0:T(1024)S(1)}, f32[1536]{0:T(1024)}, u32[]{:S(2)}) copy-start(f32[1536]{0:T(1024)} %get-tuple-element.15) | copy-start | bytes 18436
  1219.7 297.4 %copy-start.13 = (f32[1536]{0:T(1024)S(1)}, f32[1536]{0:T(1024)}, u32[]{:S(2)}) copy-start(f32[1536]{0:T(1024)} %copy-done.12) | copy-start | bytes 18436
  1219.7 297.4 %copy-start.20 = (f32[768]{0:T(1024)S(1)}, f32[768]{0:T(1024)}, u32[]{:S(2)}) copy-start(f32[768]{0:T(1024)} %copy-done.19) | copy-start | bytes 9220
  1219.7 297.4 %copy-start.27 = (f32[768]{0:T(1024)S(1)}, f32[768]{0:T(1024)}, u32[]{:S(2)}) copy-start(f32[768]{0:T(1024)} %copy-done.26) | copy-start | bytes 9220
  (22 other events, 632.0 us)
Sparse Core Ops, SparseCore 0:
  36.0 94.4 all-gather.9
  132.1 22.7 all-gather.11
  156.5 22.4 all-gather.13
  239.5 170.4 reduce-scatter.11
  411.4 38.2 all-gather.19
  451.4 95.0 all-gather.15
  548.2 38.2 all-gather.17
  588.0 37.1 all-gather.21
  627.1 95.0 all-gather.23
  785.1 170.7 reduce-scatter.15
  966.6 96.1 all-gather.25
  1064.9 40.3 reduce-scatter.31
  1107.6 39.6 reduce-scatter.29
  1149.5 39.6 reduce-scatter.27
  1191.3 31.1 reduce-scatter.21
  1224.6 30.1 reduce-scatter.23
  1257.5 31.3 reduce-scatter.25
  1291.6 31.0 reduce-scatter.19
  1325.9 93.0 reduce-scatter.17
  1421.9 95.1 reduce-scatter.13

commit v2 on v1

v2 whole, which is shorter than its diff:
```python
import functools
import jax
import jax.numpy as jnp
from jax import lax
from jax.experimental import pallas as pl
from jax.experimental.pallas import tpu as pltpu
from jax.sharding import Mesh, PartitionSpec as P

QUERY_HEADS = 16
KEY_VALUE_HEADS = 8
HEAD_SIZE = 96
SEGS = 4
BF16 = jnp.bfloat16
F32 = jnp.float32
LOG2E = 1.4426950408889634
CHUNKS = 2

rope_base = 100000.0
small_eps = 1e-05
masked_value = -1e30


def dot_f32(left, right):
    return jnp.dot(left, right, preferred_element_type=F32)


def dot_rows(left, right):
    return lax.dot_general(left, right, (((0,), (0,)), ((), ())), preferred_element_type=F32)


def dot_cols(left, right):
    return lax.dot_general(left, right, (((1,), (1,)), ((), ())), preferred_element_type=F32)


def positions(segment_ids):
    labels = jnp.arange(SEGS, dtype=jnp.int32)
    member = (segment_ids[:, None] == labels).astype(jnp.int32)
    lengths_of = jnp.sum(member, axis=0)
    earlier = (labels < segment_ids[:, None]).astype(jnp.int32)
    first_row = jnp.sum(earlier * lengths_of[None, :], axis=-1)
    return jnp.arange(segment_ids.shape[0], dtype=jnp.int32) - first_row


def rms_scale(hidden):
    return lax.rsqrt(jnp.mean(hidden * hidden, axis=-1, keepdims=True) + small_eps)


def norm_back(grad_normed, normed, inverse, gain):
    scaled = grad_normed * gain
    return inverse * (scaled - normed * jnp.mean(scaled * normed, axis=-1, keepdims=True))


def rotate_turned(values, cosine, sine_table):
    half = HEAD_SIZE // 2
    front, back = values[:half], values[half:]
    return jnp.concatenate(
        [front * cosine - back * sine_table, back * cosine + front * sine_table], axis=0
    )


def project_kernel(
    index_ref, x_ref, gain_ref, w_ref, cos_ref, sin_ref, *refs, heads, chained
):
    a_ref, turned_ref = refs[-2:]
    hidden = x_ref[...].astype(F32)
    rows = (hidden * rms_scale(hidden) * gain_ref[...]).astype(BF16)
    a_ref[...] = rows
    turned = dot_f32(rows, w_ref[...]).T
    cosine, sine_table = cos_ref[...], sin_ref[...]
    pieces = [
        rotate_turned(turned[h * HEAD_SIZE : (h + 1) * HEAD_SIZE], cosine, sine_table)
        for h in range(heads)
    ]
    pieces.append(turned[heads * HEAD_SIZE :])
    turned_ref[...] = jnp.concatenate(pieces, axis=0).astype(BF16)


def project(index, x, gain, weights, width, heads, cosine, sine_table, total_rows, previous):
    rows, model = x.shape
    block = 256 if rows % 256 == 0 else 128
    steps = rows // block
    half = HEAD_SIZE // 2
    chained = previous is not None
    operands = [index, x, gain, weights, cosine, sine_table]
    in_specs = [
        pl.BlockSpec((block, model), lambda i, at: (i, 0)),
        pl.BlockSpec((1, model), lambda i, at: (0, 0)),
        pl.BlockSpec((model, width), lambda i, at: (0, 0)),
        pl.BlockSpec((half, block), lambda i, at: (0, at[0] * steps + i)),
        pl.BlockSpec((half, block), lambda i, at: (0, at[0] * steps + i)),
    ]
    aliases = {}
    if chained:
        operands += list(previous)
        in_specs += [pl.BlockSpec(memory_space=pl.ANY)] * 2
        aliases = {6: 0, 7: 1}
    return pl.pallas_call(
        functools.partial(project_kernel, heads=heads, chained=chained),
        grid_spec=pltpu.PrefetchScalarGridSpec(
            num_scalar_prefetch=1,
            grid=(steps,),
            in_specs=in_specs,
            out_specs=[
                pl.BlockSpec((block, model), lambda i, at: (at[0] * steps + i, 0)),
                pl.BlockSpec((width, block), lambda i, at: (0, at[0] * steps + i)),
            ],
        ),
        out_shape=[
            jax.ShapeDtypeStruct((total_rows, model), BF16),
            jax.ShapeDtypeStruct((width, total_rows), BF16),
        ],
        input_output_aliases=aliases,
        name="project",
    )(*operands)


def block_mask(kv_block, q_block, block, starts, diagonal):
    keys = kv_block * block + lax.broadcasted_iota(jnp.int32, (block, starts.shape[1]), 0)
    allowed = keys >= starts
    if diagonal:
        group = starts.shape[1] // block
        lanes = lax.broadcasted_iota(jnp.int32, (1, block), 1) + q_block * block
        allowed = allowed & (keys <= jnp.concatenate([lanes] * group, axis=1))
    return allowed


def forward_kernel(
    low_ref, high_ref, start_ref, qkv_ref, out_ref, lse_ref, k_ref, vt_ref, acc_ref,
    *, heads, kv_heads, block, scale,
):
    step = pl.program_id(0)
    rows = qkv_ref.shape[1]
    group = heads // kv_heads
    factor = scale * LOG2E
    q_width = heads * HEAD_SIZE
    k_width = kv_heads * HEAD_SIZE

    @pl.when(step == 0)
    def _():
        @pl.loop(0, rows // block)
        def _(at):
            here = pl.ds(pl.multiple_of(at * block, block), block)
            for kv in range(kv_heads):
                begin = q_width + kv * HEAD_SIZE
                k_ref[kv, here, :] = qkv_ref[begin : begin + HEAD_SIZE, here].T
                begin = begin + k_width
                vt_ref[kv, :HEAD_SIZE, here] = qkv_ref[begin : begin + HEAD_SIZE, here]
                vt_ref[kv, HEAD_SIZE:, here] = jnp.ones((16, block), BF16)

    here = pl.ds(pl.multiple_of(step * block, block), block)
    starts = jnp.concatenate([start_ref[:, here]] * group, axis=1)
    turned_queries = [
        jnp.concatenate(
            [
                qkv_ref[(kv * group + g) * HEAD_SIZE : (kv * group + g + 1) * HEAD_SIZE, here]
                for g in range(group)
            ],
            axis=1,
        )
        for kv in range(kv_heads)
    ]

    def scores(kv, kv_block, masked, diagonal):
        there = pl.ds(pl.multiple_of(kv_block * block, block), block)
        raw = dot_f32(k_ref[kv, there, :], turned_queries[kv])
        if masked:
            raw = jnp.where(
                block_mask(kv_block, step, block, starts, diagonal), raw, masked_value
            )
        return raw

    def attend(kv, kv_block, probs):
        there = pl.ds(pl.multiple_of(kv_block * block, block), block)
        return dot_f32(vt_ref[kv, :, there], probs.astype(BF16))

    largest = []
    for kv in range(kv_heads):
        raw = scores(kv, step, True, True)
        top = jnp.max(raw, axis=0, keepdims=True)
        acc_ref[kv] = attend(kv, step, jnp.exp2((raw - top) * factor))
        largest.append(top)

    def more(masked):
        def body(kv_block, tops):
            result = []
            for kv in range(kv_heads):
                raw = scores(kv, kv_block, masked, False)
                top = jnp.maximum(tops[kv], jnp.max(raw, axis=0, keepdims=True))
                shrink = jnp.exp2((tops[kv] - top) * factor)
                acc_ref[kv] = acc_ref[kv] * shrink + attend(
                    kv, kv_block, jnp.exp2((raw - top) * factor)
                )
                result.append(top)
            return tuple(result)

        return body

    low = low_ref[step]
    high = jnp.minimum(high_ref[step], step)
    tops = lax.fori_loop(low, high, more(True), tuple(largest))
    tops = lax.fori_loop(jnp.maximum(low, high), step, more(False), tops)
    outs = []
    for kv in range(kv_heads):
        total = acc_ref[kv, HEAD_SIZE : HEAD_SIZE + 1, :]
        result = (acc_ref[kv, :HEAD_SIZE, :] / total).astype(BF16)
        logs = tops[kv] * factor + jnp.log2(total)
        for g in range(group):
            outs.append(result[:, g * block : (g + 1) * block])
            lse_ref[kv * group + g : kv * group + g + 1, :] = logs[:, g * block : (g + 1) * block]
    out_ref[...] = jnp.concatenate(outs, axis=0).T


def attention_forward(qkv, starts, low, high, heads, kv_heads, block):
    width, rows = qkv.shape
    q_width = heads * HEAD_SIZE
    group = heads // kv_heads
    return pl.pallas_call(
        functools.partial(
            forward_kernel, heads=heads, kv_heads=kv_heads, block=block, scale=HEAD_SIZE**-0.5
        ),
        grid_spec=pltpu.PrefetchScalarGridSpec(
            num_scalar_prefetch=2,
            grid=(rows // block,),
            in_specs=[
                pl.BlockSpec((1, rows), lambda i, *_: (0, 0)),
                pl.BlockSpec((width, rows), lambda i, *_: (0, 0)),
            ],
            out_specs=[
                pl.BlockSpec((block, q_width), lambda i, *_: (i, 0)),
                pl.BlockSpec((heads, block), lambda i, *_: (0, i)),
            ],
            scratch_shapes=[
                pltpu.VMEM((kv_heads, rows, HEAD_SIZE), BF16),
                pltpu.VMEM((kv_heads, HEAD_SIZE + 16, rows), BF16),
                pltpu.VMEM((kv_heads, HEAD_SIZE + 16, group * block), F32),
            ],
        ),
        out_shape=[
            jax.ShapeDtypeStruct((rows, q_width), BF16),
            jax.ShapeDtypeStruct((heads, rows), F32),
        ],
        name="attention_forward",
    )(low, high, starts, qkv)


def unrotate_turned(values, cosine, sine_table):
    half = HEAD_SIZE // 2
    front, back = values[:half], values[half:]
    return jnp.concatenate(
        [front * cosine + back * sine_table, back * cosine - front * sine_table], axis=0
    )


def backward_kernel(
    low_ref, high_ref, start_ref, qkv_ref, out_ref, grad_ref, lse_ref, cos_ref, sin_ref,
    result_ref, k_ref, v_ref, dk_ref, dv_ref, dq_ref, turned_ref,
    *, heads, kv_heads, block, scale,
):
    step = pl.program_id(0)
    rows = qkv_ref.shape[1]
    group = heads // kv_heads
    factor = scale * LOG2E
    q_width = heads * HEAD_SIZE
    k_width = kv_heads * HEAD_SIZE

    @pl.when(step == 0)
    def _():
        dk_ref[...] = jnp.zeros_like(dk_ref)
        dv_ref[...] = jnp.zeros_like(dv_ref)

        @pl.loop(0, rows // block)
        def _(at):
            here = pl.ds(pl.multiple_of(at * block, block), block)
            for kv in range(kv_heads):
                begin = q_width + kv * HEAD_SIZE
                k_ref[kv, here, :] = qkv_ref[begin : begin + HEAD_SIZE, here].T
                begin = begin + k_width
                v_ref[kv, here, :] = qkv_ref[begin : begin + HEAD_SIZE, here].T

    here = pl.ds(pl.multiple_of(step * block, block), block)
    starts = jnp.concatenate([start_ref[:, here]] * group, axis=1)
    turned_q = qkv_ref[:q_width, here]
    turned_grad = grad_ref[...].T
    turned_out = out_ref[...].T
    product = turned_grad.astype(F32) * turned_out.astype(F32)
    queries, queries_turned, grads, grads_turned, inners, logs = [], [], [], [], [], []
    for kv in range(kv_heads):
        pieces = [
            (slice((kv * group + g) * HEAD_SIZE, (kv * group + g + 1) * HEAD_SIZE))
            for g in range(group)
        ]
        queries_turned.append(jnp.concatenate([turned_q[s] for s in pieces], axis=1))
        grads_turned.append(jnp.concatenate([turned_grad[s] for s in pieces], axis=1))
        queries.append(jnp.concatenate([turned_q[s].T for s in pieces], axis=0))
        grads.append(jnp.concatenate([turned_grad[s].T for s in pieces], axis=0))
        inners.append(
            jnp.concatenate([jnp.sum(product[s], axis=0, keepdims=True) for s in pieces], axis=1)
        )
        logs.append(
            jnp.concatenate(
                [lse_ref[kv * group + g : kv * group + g + 1, :] for g in range(group)], axis=1
            )
        )

    def block_step(kv_block, masked, diagonal):
        there = pl.ds(pl.multiple_of(kv_block * block, block), block)
        if masked:
            allowed = block_mask(kv_block, step, block, starts, diagonal)
        for kv in range(kv_heads):
            raw = dot_f32(k_ref[kv, there, :], queries_turned[kv])
            if masked:
                raw = jnp.where(allowed, raw, masked_value)
            probs = jnp.exp2(raw * factor - logs[kv])
            grad_soft = dot_f32(v_ref[kv, there, :], grads_turned[kv])
            grad_raw = (probs * (grad_soft - inners[kv])).astype(BF16)
            dv_ref[kv, there, :] += dot_f32(probs.astype(BF16), grads[kv])
            dk_ref[kv, there, :] += dot_f32(grad_raw, queries[kv])
            k_begin = q_width + kv * HEAD_SIZE
            dq = dot_f32(qkv_ref[k_begin : k_begin + HEAD_SIZE, there], grad_raw)
            if diagonal:
                dq_ref[kv] = dq
            else:
                dq_ref[kv] += dq

    block_step(step, True, True)
    low = low_ref[step]
    high = jnp.minimum(high_ref[step], step)

    @pl.loop(low, high)
    def _(kv_block):
        block_step(kv_block, True, False)

    @pl.loop(jnp.maximum(low, high), step)
    def _(kv_block):
        block_step(kv_block, False, False)

    cosine, sine_table = cos_ref[:, here], sin_ref[:, here]
    for kv in range(kv_heads):
        for g in range(group):
            head = kv * group + g
            turned = dq_ref[kv, :, g * block : (g + 1) * block] * scale
            turned_ref[head * HEAD_SIZE : (head + 1) * HEAD_SIZE, here] = unrotate_turned(
                turned, cosine, sine_table
            ).astype(BF16)

    @pl.when(step == pl.num_programs(0) - 1)
    def _():
        @pl.loop(0, rows // block)
        def _(at):
            here = pl.ds(pl.multiple_of(at * block, block), block)
            pieces = [turned_ref[:, here]]
            for kv in range(kv_heads):
                turned = dk_ref[kv, here, :].T * scale
                pieces.append(
                    unrotate_turned(turned, cos_ref[:, here], sin_ref[:, here]).astype(
                        BF16
                    )
                )
            for kv in range(kv_heads):
                pieces.append(dv_ref[kv, here, :].T.astype(BF16))
            result_ref[here, :] = jnp.concatenate(pieces, axis=0).T


def attention_backward(
    qkv, out, grad, logs, starts, low, high, cosine, sine_table, heads, kv_heads, block
):
    width, rows = qkv.shape
    q_width = heads * HEAD_SIZE
    group = heads // kv_heads
    half = HEAD_SIZE // 2
    whole = lambda i, *_: (0, 0)
    return pl.pallas_call(
        functools.partial(
            backward_kernel, heads=heads, kv_heads=kv_heads, block=block, scale=HEAD_SIZE**-0.5
        ),
        grid_spec=pltpu.PrefetchScalarGridSpec(
            num_scalar_prefetch=2,
            grid=(rows // block,),
            in_specs=[
                pl.BlockSpec((1, rows), whole),
                pl.BlockSpec((width, rows), whole),
                pl.BlockSpec((block, q_width), lambda i, *_: (i, 0)),
                pl.BlockSpec((block, q_width), lambda i, *_: (i, 0)),
                pl.BlockSpec((heads, block), lambda i, *_: (0, i)),
                pl.BlockSpec((half, rows), whole),
                pl.BlockSpec((half, rows), whole),
            ],
            out_specs=pl.BlockSpec((rows, width), whole),
            scratch_shapes=[
                pltpu.VMEM((kv_heads, rows, HEAD_SIZE), BF16),
                pltpu.VMEM((kv_heads, rows, HEAD_SIZE), BF16),
                pltpu.VMEM((kv_heads, rows, HEAD_SIZE), F32),
                pltpu.VMEM((kv_heads, rows, HEAD_SIZE), F32),
                pltpu.VMEM((kv_heads, HEAD_SIZE, group * block), F32),
                pltpu.VMEM((q_width, rows), BF16),
            ],
        ),
        out_shape=jax.ShapeDtypeStruct((rows, width), BF16),
        name="attention_backward",
    )(low, high, starts, qkv, out, grad, logs, cosine, sine_table)


def block_bounds(starts, block):
    firsts = starts[0, ::block]
    lasts = starts[0, block - 1 :: block]
    return firsts // block, (lasts + block - 1) // block


def units_kernel(a_ref, c_ref, w_ref, hid_ref, gu_ref, dw_ref, acc_ref, *, width):
    step = pl.program_id(0)
    a, c = a_ref[...], c_ref[...]
    gate = dot_f32(a, w_ref[:, :width])
    up = dot_f32(a, w_ref[:, width : 2 * width])
    grad = dot_f32(c, w_ref[:, 2 * width :])
    sigmoid = 1.0 / (1.0 + jnp.exp(-gate))
    act = gate * sigmoid
    hid = (act * up).astype(BF16)
    dg = (grad * up * sigmoid * (1.0 + gate * (1.0 - sigmoid))).astype(BF16)
    du = (grad * act).astype(BF16)
    hid_ref[...] = hid
    gu = jnp.concatenate([dg, du], axis=1)
    gu_ref[...] = gu
    dw_gu = dot_rows(a, gu)
    dw_d = dot_rows(c, hid)
    last = pl.num_programs(0) - 1

    @pl.when(step == 0)
    def _():
        acc_ref[:, : 2 * width] = dw_gu
        acc_ref[:, 2 * width :] = dw_d

    @pl.when((step > 0) & (step < last))
    def _():
        acc_ref[:, : 2 * width] += dw_gu
        acc_ref[:, 2 * width :] += dw_d

    @pl.when(step == last)
    def _():
        dw_ref[:, : 2 * width] = (acc_ref[:, : 2 * width] + dw_gu).astype(BF16)
        dw_ref[:, 2 * width :] = (acc_ref[:, 2 * width :] + dw_d).astype(BF16)


def units(a, c, w, rows_block):
    rows, model = a.shape
    width = w.shape[1] // 3
    row_spec = pl.BlockSpec((rows_block, model), lambda i: (i, 0))
    whole = pl.BlockSpec(w.shape, lambda i: (0, 0))
    return pl.pallas_call(
        functools.partial(units_kernel, width=width),
        grid=(rows // rows_block,),
        in_specs=[row_spec, row_spec, whole],
        out_specs=[
            pl.BlockSpec((rows_block, width), lambda i: (i, 0)),
            pl.BlockSpec((rows_block, 2 * width), lambda i: (i, 0)),
            whole,
        ],
        out_shape=[
            jax.ShapeDtypeStruct((rows, width), BF16),
            jax.ShapeDtypeStruct((rows, 2 * width), BF16),
            jax.ShapeDtypeStruct(w.shape, BF16),
        ],
        scratch_shapes=[pltpu.VMEM(w.shape, F32)],
        name="units",
    )(a, c, w)


def sum_kernel(*refs, count):
    total = dot_cols(refs[0][...], refs[count][...])
    for at in range(1, count):
        total += dot_cols(refs[at][...], refs[count + at][...])
    refs[-1][...] = total.astype(refs[-1].dtype)


def sum_products(lefts, rights, begin, rows, first, part, dtype, rows_block):
    model = rights[0].shape[0]
    depth = lefts[0].shape[1]
    offset = begin // rows_block
    return pl.pallas_call(
        functools.partial(sum_kernel, count=len(lefts)),
        grid=(rows // rows_block,),
        in_specs=[pl.BlockSpec((rows_block, depth), lambda i: (i + offset, 0)) for _ in lefts]
        + [
            pl.BlockSpec((model, depth), lambda i: (0, part), pipeline_mode=pl.Buffered(1))
            for _ in rights
        ],
        out_specs=pl.BlockSpec((rows_block, model), lambda i: (i, 0)),
        out_shape=jax.ShapeDtypeStruct((rows, model), dtype),
        name="sum_products",
    )(*lefts, *rights)


def on_device(
    tokens,
    cotangent,
    seg_ids,
    gain_attn,
    gain_ffn,
    w_query,
    w_key,
    value_projection,
    w_out,
    w_gate,
    w_up,
    w_down,
    *,
    planes,
    lanes,
):
    core = lax.axis_index("core")
    place = lax.axis_index("tensor")
    first_core = core == 0
    phases = lanes.bit_length() - 1
    bits = [1 << k for k in range(phases)]
    orders = (bits, bits[::-1])
    tables = [
        [sum(order[k] for k in range(phases) if slot >> k & 1) for slot in range(lanes)]
        for order in orders
    ]
    mirror = [tables[1].index(offset) for offset in tables[0]]
    natural = [
        place ^ jnp.where(first_core, tables[0][slot], tables[1][slot]) for slot in range(lanes)
    ]

    def swap(value):
        return lax.ppermute(value, "core", [(0, 1), (1, 0)])

    def exchange(value, offsets):
        pairs = [
            (c * lanes + i, c * lanes + (i ^ offsets[c])) for c in range(2) for i in range(lanes)
        ]
        return lax.ppermute(value, ("core", "tensor"), pairs)

    def hop(value, phase):
        return exchange(value, [order[phase] for order in orders])

    def to_slot(value, slot):
        if slot == 0:
            return value
        return exchange(value, [table[slot] for table in tables])

    def spread(value):
        have = [value]
        for phase in range(phases):
            have = have + [hop(v, phase) for v in have]
        return have

    def collect(slots):
        have = list(slots)
        for phase in reversed(range(phases)):
            half = 1 << phase
            arrived = [hop(have[half + at], phase) for at in range(half)]
            have = [
                have[at].astype(F32) + arrived[at].astype(F32) for at in range(half)
            ]
            if phase > 0:
                have = [v.astype(BF16) for v in have]
        return have[0]

    def mine(value, axis):
        return lax.dynamic_index_in_dim(value, core, axis, keepdims=False)

    def theirs(value, axis):
        return lax.dynamic_index_in_dim(value, 1 - core, axis, keepdims=False)

    def by_core(own, other):
        return jnp.where(first_core, own, other), jnp.where(first_core, other, own)

    rows, model = tokens.shape
    shard = w_query.shape[0]
    pack_rows = seg_ids.shape[1]
    q_width = w_query.shape[1]
    k_width = w_key.shape[1]
    width = q_width + 2 * k_width
    heads = q_width // HEAD_SIZE
    kv_heads = k_width // HEAD_SIZE

    token_slots = spread(tokens)
    gains = jnp.pad(jnp.stack([gain_attn, gain_ffn], axis=1), ((0, 0), (0, 126)))
    attn_weights = lax.all_gather(
        jnp.concatenate([w_query, w_key, value_projection, w_out.T, gains], axis=1),
        ("z", "core"),
        axis=0,
        tiled=True,
    )
    cotangent_pair = jnp.concatenate([cotangent, swap(cotangent)], axis=0)
    units_local = w_gate.shape[1]
    part = units_local // (2 * CHUNKS)
    stacked = jnp.stack([w_gate, w_up, w_down.T], axis=1).reshape(shard, 3, 2, CHUNKS, part)
    kept = mine(stacked, 2)
    arrived = swap(theirs(stacked, 2))
    unit_weights = []
    for chunk in range(CHUNKS):
        low_rows, high_rows = by_core(
            kept[:, :, chunk].reshape(shard, 3 * part),
            arrived[:, :, chunk].reshape(shard, 3 * part),
        )
        gathered = lax.all_gather(
            jnp.concatenate([low_rows, high_rows], axis=0), "z", axis=0, tiled=True
        )
        unit_weights.append(spread(gathered))

    gain_rows = attn_weights[:, width + q_width : width + q_width + 2].astype(F32).T
    gain_one, gain_two = gain_rows[0:1], gain_rows[1:2]
    out_own = attn_weights[:, width : width + q_width].reshape(planes, 2, shard, q_width)
    out_mine = spread(mine(out_own, 1).reshape(planes * shard, q_width))
    out_theirs = [theirs(out_own, 1).reshape(planes * shard, q_width)] + [
        swap(out_mine[mirror[slot]]) for slot in range(1, lanes)
    ]
    out_weights = []
    for own, other in zip(out_mine, out_theirs):
        low_rows, high_rows = by_core(own, other)
        out_weights.append(
            jnp.stack(
                [
                    low_rows.reshape(planes, shard, q_width),
                    high_rows.reshape(planes, shard, q_width),
                ],
                axis=1,
            ).reshape(model, q_width)
        )
    out_weights = jnp.concatenate(out_weights, axis=1)

    segment_row = seg_ids[0]
    position_ids = positions(segment_row)
    frequency = rope_base ** (-jnp.arange(HEAD_SIZE // 2, dtype=F32) * 2.0 / HEAD_SIZE)
    phase_angle = position_ids.astype(F32)[None, :] * frequency[:, None]
    cosine, sine_table = jnp.cos(phase_angle), jnp.sin(phase_angle)
    starts = (jnp.arange(pack_rows, dtype=jnp.int32) - position_ids)[None, :]
    low_512, high_512 = block_bounds(starts, 512)
    low_256, high_256 = block_bounds(starts, 256)
    projected = None
    for slot in range(lanes):
        projected = project(
            natural[slot][None].astype(jnp.int32),
            token_slots[slot],
            gain_one,
            attn_weights,
            width,
            heads + kv_heads,
            cosine,
            sine_table,
            pack_rows,
            projected,
        )
    attn_rows, qkv = projected
    attn_out, log_totals = attention_forward(
        qkv, starts, low_512, high_512, heads, kv_heads, 512
    )
    out_slots = [
        to_slot(lax.dynamic_slice_in_dim(attn_out, natural[slot] * rows, rows, 0), slot)
        for slot in range(lanes)
    ]
    out_rows = jnp.concatenate(out_slots, axis=1)
    hidden_in = tokens.astype(F32)
    inverse_one = rms_scale(hidden_in)
    normed_one = hidden_in * inverse_one
    hidden_mid = hidden_in + dot_cols(out_rows, out_weights)
    inverse_two = rms_scale(hidden_mid)
    normed_two = hidden_mid * inverse_two
    ffn_input = (normed_two * gain_two).astype(BF16)
    ffn_pair = jnp.concatenate([ffn_input, swap(ffn_input)], axis=0)

    unit_rows = 768 if (2 * rows) % 768 == 0 else 2 * rows
    hids, grads, unit_grads = [], [], [[] for _ in range(CHUNKS)]
    weights_used = []
    for slot in range(lanes):
        for chunk in range(CHUNKS):
            weight = unit_weights[chunk][slot]
            hid, grad, grad_w = units(ffn_pair, cotangent_pair, weight, unit_rows)
            hids.append(hid)
            grads.append(grad)
            weights_used.append(weight)
            unit_grads[chunk].append(grad_w)
    sum_rows = 256 if rows % 256 == 0 else 128
    their_grad = swap(
        sum_products(grads, weights_used, rows, rows, 0, 0, F32, sum_rows)
    )
    my_grad = sum_products(grads, weights_used, 0, rows, 0, 0, F32, sum_rows)
    grad_ffn_input = my_grad + their_grad
    their_sum = swap(sum_products(hids, weights_used, rows, rows, 0, 2, BF16, sum_rows))
    my_sum = sum_products(hids, weights_used, 0, rows, 0, 2, F32, sum_rows)
    result = (hidden_mid + (my_sum + their_sum.astype(F32))).astype(BF16)

    grad_mid = cotangent.astype(F32) + norm_back(
        grad_ffn_input, normed_two, inverse_two, gain_two
    )
    gain_two_part = jnp.sum(grad_ffn_input * normed_two, axis=0)
    grad_branch = grad_mid.astype(BF16)

    grad_out_rows = dot_f32(grad_branch, out_weights).astype(BF16)
    grad_attended = jnp.zeros((pack_rows, q_width), BF16)
    for slot in range(lanes):
        piece = to_slot(grad_out_rows[:, slot * q_width : (slot + 1) * q_width], slot)
        grad_attended = lax.dynamic_update_slice_in_dim(
            grad_attended, piece, natural[slot] * rows, 0
        )
    grad_out_w = (
        dot_rows(grad_branch, out_rows).astype(BF16).reshape(planes, 2, shard, lanes, q_width)
    )
    sent = theirs(grad_out_w, 1)
    sent = swap(jnp.stack([sent[:, :, mirror[slot]] for slot in range(lanes)], axis=2))
    grad_out_w = (mine(grad_out_w, 1).astype(F32) + sent.astype(F32)).astype(BF16)
    grad_out_w = collect(
        [grad_out_w[:, :, slot].reshape(planes * shard, q_width) for slot in range(lanes)]
    )
    grad_out_w = lax.psum_scatter(
        grad_out_w.astype(BF16), "z", scatter_dimension=0, tiled=True
    )
    grad_qkv = attention_backward(
        qkv,
        attn_out,
        grad_attended,
        log_totals,
        starts,
        low_256,
        high_256,
        cosine,
        sine_table,
        heads,
        kv_heads,
        256,
    )
    projection = attn_weights[:, :width]
    grad_slots = [
        dot_cols(
            lax.dynamic_slice_in_dim(grad_qkv, natural[slot] * rows, rows, 0), projection
        ).astype(BF16)
        for slot in range(lanes)
    ]
    grad_attn_input = collect(grad_slots)
    grad_qkv_w = lax.psum_scatter(
        dot_rows(attn_rows, grad_qkv).astype(BF16),
        ("z", "core"),
        scatter_dimension=0,
        tiled=True,
    ).astype(F32)
    grad_tokens = grad_mid + norm_back(grad_attn_input, normed_one, inverse_one, gain_one)
    gain_one_part = jnp.sum(grad_attn_input * normed_one, axis=0)

    unit_pieces = []
    for chunk in range(CHUNKS):
        summed = collect(unit_grads[chunk]).astype(BF16)
        scattered = lax.psum_scatter(summed, "z", scatter_dimension=0, tiled=True)
        scattered = scattered.reshape(2, shard, 3, part)
        low_part, high_part = by_core(mine(scattered, 0), swap(theirs(scattered, 0)))
        unit_pieces.append((low_part, high_part))
    unit_w = jnp.concatenate(
        [piece[0] for piece in unit_pieces] + [piece[1] for piece in unit_pieces], axis=2
    ).astype(F32)
    gain_sums = lax.psum(
        jnp.stack([gain_one_part, gain_two_part]), ("z", "core", "tensor")
    )
    owner = lax.axis_index("z") * 2 + core
    gain_sums = lax.dynamic_slice_in_dim(gain_sums, owner * shard, shard, 1)
    return (
        result,
        grad_tokens,
        gain_sums[0],
        gain_sums[1],
        grad_qkv_w[:, :q_width],
        grad_qkv_w[:, q_width : q_width + k_width],
        grad_qkv_w[:, q_width + k_width :],
        grad_out_w.astype(F32).T,
        unit_w[:, 0],
        unit_w[:, 1],
        unit_w[:, 2].T,
    )


def solution(mesh):
    packs, lanes = mesh.shape["dp"], mesh.shape["tensor"]
    split_mesh = Mesh(mesh.devices.reshape(packs // 2, 2, lanes), ("z", "core", "tensor"))
    dp = ("z", "core")
    everywhere = ("z", "core", "tensor")
    return jax.shard_map(
        functools.partial(on_device, planes=packs // 2, lanes=lanes),
        mesh=split_mesh,
        in_specs=(
            P(everywhere, None),
            P(everywhere, None),
            P(dp, None),
            P(dp),
            P(dp),
            P(dp, "tensor"),
            P(dp, "tensor"),
            P(dp, "tensor"),
            P("tensor", dp),
            P(dp, "tensor"),
            P(dp, "tensor"),
            P("tensor", dp),
        ),
        out_specs=(
            P(everywhere, None),
            P(everywhere, None),
            P(dp),
            P(dp),
            P(dp, "tensor"),
            P(dp, "tensor"),
            P(dp, "tensor"),
            P("tensor", dp),
            P(dp, "tensor"),
            P(dp, "tensor"),
            P("tensor", dp),
        ),
        check_vma=False,
    )
```

time: 1540 us -> 863 us (0.56)
  waiting for transfers between devices: 983 us -> 279 us
  matrix products: 277 us -> 46.9 us
  Pallas kernels: 91.7 us -> 284 us
  starting transfers between devices: 1.27 us -> 51.2 us
  local copies, waits for them, and re-layouts: 17.6 us -> 66.2 us
  blocking collectives: 80.1 us -> 39.5 us
    reduce_scatter x11 -> x4, waiting for transfers between devices: 592 us -> 15.1 us  [the longest x1 15 us: on_device(): lax.psum_scatter(grad_out_w.astype(BF16), 'z', scatter_dimension=0, tiled...]
    all_gather x9 -> x3, waiting for transfers between devices: 388 us -> 0.01 us  [the longest x2 0.01 us: on_device(): lax.all_gather(jnp.concatenate([low_rows, high_rows], axis=0), 'z', axis=...]
    ppermute x0 -> x41, waiting for transfers between devices: none -> 263 us  [the longest x30 262 us: exchange(): return lax.ppermute(value, ('core', 'tensor'), pairs)]
    pallas_call x0 -> x16, Pallas kernels: none -> 208 us  [the longest x8 128 us: units(): pl.pallas_call(functools.partial(units_kernel, width=width), grid=(rows /...]
    dot_general x7 -> x5, matrix products: 111 us -> 22.6 us  [dot_cols(): lax.dot_general(left, right, (((1,), (1,)), ((), ())), preferred_element_...]
    dot_general x7 -> x1, matrix products: 83.4 us -> 4.5 us  [dot_f32(): return jnp.dot(left, right, preferred_element_type=F32)]
    dot_general x7 -> x2, matrix products: 82.4 us -> 19.9 us  [dot_rows(): lax.dot_general(left, right, (((0,), (0,)), ((), ())), preferred_element_...]
    ppermute x0 -> x41, starting transfers between devices: none -> 50.7 us  [the longest x30 40.5 us: exchange(): return lax.ppermute(value, ('core', 'tensor'), pairs)]
  transfers between devices with their start and end apart: 20 -> 48, of which waited for: 15 -> 15; matrix products, arithmetic and copies ran while one was open for 17% -> 20% of each run, Pallas kernels for 6% -> 33%
where the time goes in v2:
time: 863 us; the launch traced here: 854 us
  Pallas kernels  284 us (33%)
  waiting for transfers between devices  279 us (32%)
  other arithmetic  72.3 us (8%)
  local copies, waits for them, and re-layouts  66.2 us (8%)
  starting transfers between devices  51.2 us (6%)
  matrix products  46.9 us (5%)
  blocking collectives  39.5 us (5%)
  between operations  15.3 us (2%)
    ppermute x30, waiting for transfers between devices, exchange(): return lax.ppermute(value, ('core', 'tensor'), pairs)  262 us
    pallas_call x8, Pallas kernels, units(): pl.pallas_call(functools.partial(units_kernel, width=width), grid=(rows /...  128 us
    pallas_call x4, Pallas kernels, sum_products(): pl.pallas_call(functools.partial(sum_kernel, count=len(lefts)), grid=(row...  54.7 us
    pallas_call x1, Pallas kernels, attention_backward(): pl.pallas_call(functools.partial(backward_kernel, heads=heads, kv_heads=k...  47.2 us
    ppermute x30, starting transfers between devices, exchange(): return lax.ppermute(value, ('core', 'tensor'), pairs)  40.5 us
    psum x1, blocking collectives, on_device(): lax.psum(jnp.stack([gain_one_part, gain_two_part]), ('z', 'core', 'tensor'))  39.5 us
    pallas_call x1, Pallas kernels, attention_forward(): pl.pallas_call(functools.partial(forward_kernel, heads=heads, kv_heads=kv...  28.9 us
    pallas_call x4, Pallas kernels, project(): pl.pallas_call(functools.partial(project_kernel, heads=heads, chained=cha...  25.3 us
  transfers between devices with their start and end apart: 48, of which 15 were waited for; matrix products, arithmetic and copies ran while one was open for 20% of the time, Pallas kernels for 33%

profile of v2, /device:TPU:0, one launch (start us, length us, event | category | flops | bytes accessed | tf_op | source)
XLA Modules:
  0.0 854.2 jit_solution(7173037836166229479)
XLA Ops:
  21.6 49.5 %collective-permute-done.x_ref = bf16[768,1536]{1,0:T(8,128)(2,1)} collective-permute-done((bf16[768,1536]{1,0:T(8,128)(2,1)S(1)}, bf16[768,1536]{1,0:T(8,128)(2,1)}, u32[]{:S(2)}, u32[]{:S(2)}) %collective-permute-start) | collective-permute-done | bytes 2359328 | tf_op jit(solution)/shard_map/ppermute | solution.py:531
  85.1 12.6 %collective-permute-done.6 = bf16[768,384]{1,0:T(8,128)(2,1)} collective-permute-done((bf16[768,384]{1,0:T(8,128)(2,1)}, bf16[768,384]{1,0:T(8,128)(2,1)}, u32[]{:S(2)}, u32[]{:S(2)}) %collective-permute-start.6) | collective-permute-done | bytes 589856 | tf_op jit(solution)/shard_map/ppermute | solution.py:531
  98.0 15.1 %collective-permute-done.7 = bf16[768,384]{1,0:T(8,128)(2,1)} collective-permute-done((bf16[768,384]{1,0:T(8,128)(2,1)}, bf16[768,384]{1,0:T(8,128)(2,1)}, u32[]{:S(2)}, u32[]{:S(2)}) %collective-permute-start.7) | collective-permute-done | bytes 589856 | tf_op jit(solution)/shard_map/ppermute | solution.py:531
  142.2 28.9 %attention_forward.1 = (bf16[3072,384]{1,0:T(8,128)(2,1)}, f32[4,3072]{1,0:T(4,128)}) custom-call(s32[6]{0:T(128)} %get-tuple-element.143.low_ref, s32[6]{0:T(128)} %get-tuple-element.142.high_ref, s32[1,3072]{1,0:T(1,128)} %copy-done.23, bf16[768,3072]{1,0:T(8,128)(2,1)} %get-tuple-element.51.qkv_ref), custom_call_target="tpu_custom_call" | custom-call | tf_op jit(solution)/shard_map/attention_forward/pallas_call | solution.py:217
  191.1 12.5 %collective-permute-done.4 = bf16[768,384]{1,0:T(8,128)(2,1)} collective-permute-done((bf16[768,384]{1,0:T(8,128)(2,1)}, bf16[768,384]{1,0:T(8,128)(2,1)}, u32[]{:S(2)}, u32[]{:S(2)}) %collective-permute-start.4) | collective-permute-done | bytes 589856 | tf_op jit(solution)/shard_map/ppermute | solution.py:531
  203.7 6.7 multiply_reduce_fusion.2
  216.4 12.7 %collective-permute-done.15.w_ref.refs_10_ = bf16[1536,768]{1,0:T(8,128)(2,1)} collective-permute-done((bf16[1536,768]{1,0:T(8,128)(2,1)}, bf16[1536,768]{1,0:T(8,128)(2,1)}, u32[]{:S(2)}, u32[]{:S(2)}) %collective-permute-start.15) | collective-permute-done | bytes 2359328 | tf_op jit(solution)/shard_map/ppermute | solution.py:531
  234.4 42.4 %collective-permute-done.16.w_ref.refs_11_ = bf16[1536,768]{1,0:T(8,128)(2,1)} collective-permute-done((bf16[1536,768]{1,0:T(8,128)(2,1)}, bf16[1536,768]{1,0:T(8,128)(2,1)}, u32[]{:S(2)}, u32[]{:S(2)}) %collective-permute-start.16) | collective-permute-done | bytes 2359328 | tf_op jit(solution)/shard_map/ppermute | solution.py:531
  284.4 15.8 %units.14 = (bf16[1536,256]{1,0:T(8,128)(2,1)}, bf16[1536,512]{1,0:T(8,128)(2,1)}, bf16[1536,768]{1,0:T(8,128)(2,1)}) custom-call(bf16[1536,1536]{1,0:T(8,128)(2,1)} %pad_maximum_fusion.1.a_ref, bf16[1536,1536]{1,0:T(8,128)(2,1)} %constant_dynamic-update-slice_fusion.c_ref, bf16[1536,768]{1,0:T(8,128)(2,1)} %collective-permute-done.19.w_ref.refs_14_), custom_call_target="tpu_custom_call" | custom-call | tf_op jit(solution)/shard_map/units/pallas_call | solution.py:448
  300.4 16.4 %units.10 = (bf16[1536,256]{1,0:T(8,128)(2,1)}, bf16[1536,512]{1,0:T(8,128)(2,1)}, bf16[1536,768]{1,0:T(8,128)(2,1)}) custom-call(bf16[1536,1536]{1,0:T(8,128)(2,1)} %pad_maximum_fusion.1.a_ref, bf16[1536,1536]{1,0:T(8,128)(2,1)} %constant_dynamic-update-slice_fusion.c_ref, bf16[1536,768]{1,0:T(8,128)(2,1)} %collective-permute-done.15.w_ref.refs_10_), custom_call_target="tpu_custom_call" | custom-call | tf_op jit(solution)/shard_map/units/pallas_call | solution.py:448
  316.7 15.9 %units.8 = (bf16[1536,256]{1,0:T(8,128)(2,1)}, bf16[1536,512]{1,0:T(8,128)(2,1)}, bf16[1536,768]{1,0:T(8,128)(2,1)}) custom-call(bf16[1536,1536]{1,0:T(8,128)(2,1)} %pad_maximum_fusion.1.a_ref, bf16[1536,1536]{1,0:T(8,128)(2,1)} %constant_dynamic-update-slice_fusion.c_ref, bf16[1536,768]{1,0:T(8,128)(2,1)} %all-gather.6.cloned.1.call-done.w_ref.refs_8_), custom_call_target="tpu_custom_call" | custom-call | tf_op jit(solution)/shard_map/units/pallas_call | solution.py:448
  332.6 16.0 %units.11 = (bf16[1536,256]{1,0:T(8,128)(2,1)}, bf16[1536,512]{1,0:T(8,128)(2,1)}, bf16[1536,768]{1,0:T(8,128)(2,1)}) custom-call(bf16[1536,1536]{1,0:T(8,128)(2,1)} %pad_maximum_fusion.1.a_ref, bf16[1536,1536]{1,0:T(8,128)(2,1)} %constant_dynamic-update-slice_fusion.c_ref, bf16[1536,768]{1,0:T(8,128)(2,1)} %collective-permute-done.16.w_ref.refs_11_), custom_call_target="tpu_custom_call" | custom-call | tf_op jit(solution)/shard_map/units/pallas_call | solution.py:448
  348.7 15.9 %units.9 = (bf16[1536,256]{1,0:T(8,128)(2,1)}, bf16[1536,512]{1,0:T(8,128)(2,1)}, bf16[1536,768]{1,0:T(8,128)(2,1)}) custom-call(bf16[1536,1536]{1,0:T(8,128)(2,1)} %pad_maximum_fusion.1.a_ref, bf16[1536,1536]{1,0:T(8,128)(2,1)} %constant_dynamic-update-slice_fusion.c_ref, bf16[1536,768]{1,0:T(8,128)(2,1)} %all-gather.8.cloned.1.call-done.w_ref.refs_9_), custom_call_target="tpu_custom_call" | custom-call | tf_op jit(solution)/shard_map/units/pallas_call | solution.py:448
  364.6 16.1 %units.12 = (bf16[1536,256]{1,0:T(8,128)(2,1)}, bf16[1536,512]{1,0:T(8,128)(2,1)}, bf16[1536,768]{1,0:T(8,128)(2,1)}) custom-call(bf16[1536,1536]{1,0:T(8,128)(2,1)} %pad_maximum_fusion.1.a_ref, bf16[1536,1536]{1,0:T(8,128)(2,1)} %constant_dynamic-update-slice_fusion.c_ref, bf16[1536,768]{1,0:T(8,128)(2,1)} %collective-permute-done.17.w_ref.refs_12_), custom_call_target="tpu_custom_call" | custom-call | tf_op jit(solution)/shard_map/units/pallas_call | solution.py:448
  380.7 15.8 %units.15 = (bf16[1536,256]{1,0:T(8,128)(2,1)}, bf16[1536,512]{1,0:T(8,128)(2,1)}, bf16[1536,768]{1,0:T(8,128)(2,1)}) custom-call(bf16[1536,1536]{1,0:T(8,128)(2,1)} %pad_maximum_fusion.1.a_ref, bf16[1536,1536]{1,0:T(8,128)(2,1)} %constant_dynamic-update-slice_fusion.c_ref, bf16[1536,768]{1,0:T(8,128)(2,1)} %collective-permute-done.20.w_ref.refs_15_), custom_call_target="tpu_custom_call" | custom-call | tf_op jit(solution)/shard_map/units/pallas_call | solution.py:448
  396.5 16.3 %units.13 = (bf16[1536,256]{1,0:T(8,128)(2,1)}, bf16[1536,512]{1,0:T(8,128)(2,1)}, bf16[1536,768]{1,0:T(8,128)(2,1)}) custom-call(bf16[1536,1536]{1,0:T(8,128)(2,1)} %pad_maximum_fusion.1.a_ref, bf16[1536,1536]{1,0:T(8,128)(2,1)} %constant_dynamic-update-slice_fusion.c_ref, bf16[1536,768]{1,0:T(8,128)(2,1)} %collective-permute-done.18.w_ref.refs_13_), custom_call_target="tpu_custom_call" | custom-call | tf_op jit(solution)/shard_map/units/pallas_call | solution.py:448
  412.8 17.2 %sum_products.7 = f32[768,1536]{1,0:T(8,128)} custom-call(bf16[1536,512]{1,0:T(8,128)(2,1)} %get-tuple-element.61.refs_0_, bf16[1536,512]{1,0:T(8,128)(2,1)} %get-tuple-element.62.refs_1_, bf16[1536,512]{1,0:T(8,128)(2,1)} %get-tuple-element.63.refs_2_, bf16[1536,512]{1,0:T(8,128)(2,1)} %get-tuple-element.64.refs_3_, ...), custom_call_target="tpu_custom_call" | custom-call | tf_op jit(solution)/shard_map/sum_products/pallas_call | solution.py:478
  439.5 9.9 %sum_products.5 = bf16[768,1536]{1,0:T(8,128)(2,1)} custom-call(bf16[1536,256]{1,0:T(8,128)(2,1)} %get-tuple-element.53.refs_0_, bf16[1536,256]{1,0:T(8,128)(2,1)} %get-tuple-element.54.refs_1_, bf16[1536,256]{1,0:T(8,128)(2,1)} %get-tuple-element.55.refs_2_, bf16[1536,256]{1,0:T(8,128)(2,1)} %get-tuple-element.56.refs_3_, ...), custom_call_target="tpu_custom_call" | custom-call | tf_op jit(solution)/shard_map/sum_products/pallas_call | solution.py:478
  449.4 10.2 %sum_products.4 = f32[768,1536]{1,0:T(8,128)} custom-call(bf16[1536,256]{1,0:T(8,128)(2,1)} %get-tuple-element.53.refs_0_, bf16[1536,256]{1,0:T(8,128)(2,1)} %get-tuple-element.54.refs_1_, bf16[1536,256]{1,0:T(8,128)(2,1)} %get-tuple-element.55.refs_2_, bf16[1536,256]{1,0:T(8,128)(2,1)} %get-tuple-element.56.refs_3_, ...), custom_call_target="tpu_custom_call" | custom-call | tf_op jit(solution)/shard_map/sum_products/pallas_call | solution.py:478
  459.6 17.4 %sum_products.6 = f32[768,1536]{1,0:T(8,128)} custom-call(bf16[1536,512]{1,0:T(8,128)(2,1)} %get-tuple-element.61.refs_0_, bf16[1536,512]{1,0:T(8,128)(2,1)} %get-tuple-element.62.refs_1_, bf16[1536,512]{1,0:T(8,128)(2,1)} %get-tuple-element.63.refs_2_, bf16[1536,512]{1,0:T(8,128)(2,1)} %get-tuple-element.64.refs_3_, ...), custom_call_target="tpu_custom_call" | custom-call | tf_op jit(solution)/shard_map/sum_products/pallas_call | solution.py:478
  483.3 26.6 %collective-permute-done.33 = bf16[1536,768]{1,0:T(8,128)(2,1)} collective-permute-done((bf16[1536,768]{1,0:T(8,128)(2,1)}, bf16[1536,768]{1,0:T(8,128)(2,1)}, u32[]{:S(2)}, u32[]{:S(2)}) %collective-permute-start.33) | collective-permute-done | bytes 2359328 | tf_op jit(solution)/shard_map/ppermute | solution.py:531
  517.0 7.3 multiply_reduce_fusion
  524.3 9.9 %multiply_add_fusion = (f32[768,1536]{1,0:T(8,128)S(1)}, bf16[768,1536]{1,0:T(8,128)(2,1)}) fusion(bf16[768,1536]{1,0:T(8,128)(2,1)S(1)} %copy-done.9, f32[768,1536]{1,0:T(8,128)} %copy-done.3, f32[768]{0:T(1024)S(1)} %broadcast_multiply_fusion.1, f32[1536]{0:T(1024)S(1)} %get-tuple-element.84, f32[768]{0:T(1024)S(1)} %add_rsqrt_fusion.1, ...), kind=kLoop, calls=%fused_computation.27 | loop fusion | flops 14155776 | bytes 30683136 | tf_op jit(solution)/shard_map/add | solution.py:684
  536.5 7.0 convolution_convert_fusion
  543.4 9.0 %reshape.138 = bf16[4,2,192,4,384]{4,3,2,1,0:T(4,128)(2,1)} reshape(bf16[1536,1536]{1,0:T(8,128)(2,1)} %convolution_convert_fusion) | data formatting | bytes 9437184 | tf_op jit(solution)/shard_map/reshape | solution.py:698
  596.7 47.2 %attention_backward.1 = bf16[3072,768]{1,0:T(8,128)(2,1)} custom-call(s32[12]{0:T(128)} %get-tuple-element.141.low_ref, s32[12]{0:T(128)} %get-tuple-element.140.high_ref, s32[1,3072]{1,0:T(1,128)} %copy-done.23, bf16[768,3072]{1,0:T(8,128)(2,1)} %get-tuple-element.51.qkv_ref, bf16[3072,384]{1,0:T(8,128)(2,1)} %get-tuple-element.52.out_ref, ...), custom_call_target="tpu_custom_call" | custom-call | tf_op jit(solution)/shard_map/attention_backward/pallas_call | solution.py:372
  660.9 22.2 %collective-permute-done.31 = bf16[768,384]{1,0:T(8,128)(2,1)S(1)} collective-permute-done((bf16[768,384]{1,0:T(8,128)(2,1)S(1)}, bf16[768,384]{1,0:T(8,128)(2,1)S(1)}, u32[]{:S(2)}, u32[]{:S(2)}) %collective-permute-start.31) | collective-permute-done | bytes 589856 | tf_op jit(solution)/shard_map/ppermute | solution.py:531
  687.4 54.0 %collective-permute-done.30 = bf16[768,384]{1,0:T(8,128)(2,1)S(1)} collective-permute-done((bf16[768,384]{1,0:T(8,128)(2,1)S(1)}, bf16[768,384]{1,0:T(8,128)(2,1)S(1)}, u32[]{:S(2)}, u32[]{:S(2)}) %collective-permute-start.30) | collective-permute-done | bytes 589856 | tf_op jit(solution)/shard_map/ppermute | solution.py:531
  742.6 12.9 %convolution_convert_fusion.1 = bf16[1536,768]{1,0:T(8,128)(2,1)} fusion(bf16[3072,1536]{1,0:T(8,128)(2,1)} %get-tuple-element.70, bf16[3072,768]{1,0:T(8,128)(2,1)} %attention_backward.1), kind=kOutput, calls=%fused_computation.33 | convolution fusion | flops 7248936960 | bytes 16515072 | tf_op jit(solution)/shard_map/dot_general | solution.py:28
  768.0 15.0 %reduce-scatter.7.cloned.1.call-done = bf16[192,384]{1,0:T(8,128)(2,1)} async-done(((bf16[768,384]{1,0:T(8,128)(2,1)}), bf16[192,384]{1,0:T(8,128)(2,1)}) %reduce-scatter.7.cloned.1.call-update) | async-done | bytes 147472 | tf_op jit(solution)/shard_map/reduce_scatter | solution.py:706
  796.6 39.5 %psum.7 = f32[2,1536]{1,0:T(2,128)S(1)} all-reduce(f32[2,1536]{1,0:T(2,128)S(1)} %pad_maximum_fusion.14), channel_id=1, replica_groups=mesh['z'=4,'core'=2,'tensor'=4] {'z','core','tensor'}, use_global_device_ids=true, to_apply=%region_8.9 | all-reduce | flops 3072 | bytes 24576 | tf_op jit(solution)/shard_map/psum | solution.py:750
  836.7 6.8 fusion.6
  (255 shorter events, 218.2 us)
Async XLA Ops:
  7.2 71.4 %all-gather.4.cloned.1.call-start = ((), (), s32[]{:S(2)}) async-start(), calls=%async_computation.4 | async-start | bytes 4423680 | tf_op jit(solution)/shard_map/all_gather | solution.py:579
  10.8 175.0 %all-gather.6.cloned.1.call-start = ((), (), s32[]{:S(2)}) async-start(), calls=%async_computation.5 | async-start | bytes 2949120 | tf_op jit(solution)/shard_map/all_gather | solution.py:597
  16.8 172.2 %all-gather.8.cloned.1.call-start = ((), (), s32[]{:S(2)}) async-start(), calls=%async_computation.6 | async-start | bytes 2949120 | tf_op jit(solution)/shard_map/all_gather | solution.py:597
  16.9 54.1 %collective-permute-start = (bf16[768,1536]{1,0:T(8,128)(2,1)S(1)}, bf16[768,1536]{1,0:T(8,128)(2,1)}, u32[]{:S(2)}, u32[]{:S(2)}) collective-permute-start(bf16[768,1536]{1,0:T(8,128)(2,1)S(1)} %copy-done.4), channel_id=1, source_target_pairs={{0,1},{1,0},{2,3},{3,2},{4,6},{5,7},{6,4},{7,5},{8,9},{9,8},{10,11... | collective-permute-start | bytes 7077896 | tf_op jit(solution)/shard_map/ppermute | solution.py:531
  19.8 109.8 %collective-permute-start.2 = (bf16[768,1536]{1,0:T(8,128)(2,1)S(1)}, bf16[768,1536]{1,0:T(8,128)(2,1)}, u32[]{:S(2)}, u32[]{:S(2)}) collective-permute-start(bf16[768,1536]{1,0:T(8,128)(2,1)S(1)} %copy-done.4), channel_id=1, source_target_pairs={{0,2},{1,3},{2,0},{3,1},{4,5},{5,4},{6,7},{7,6},{8,10},{9,11},{10,... | collective-permute-start | bytes 7077896 | tf_op jit(solution)/shard_map/ppermute | solution.py:531
  21.3 211.3 %collective-permute-start.13 = (bf16[768,1536]{1,0:T(8,128)(2,1)}, bf16[768,1536]{1,0:T(8,128)(2,1)}, u32[]{:S(2)}, u32[]{:S(2)}) collective-permute-start(bf16[768,1536]{1,0:T(8,128)(2,1)} %param.13), channel_id=1, source_target_pairs={{0,4},{4,0},{1,5},{5,1},{2,6},{6,2},{3,7},{7,3},{8,12},{12,8},{9,1... | collective-permute-start | bytes 7077896 | tf_op jit(solution)/shard_map/ppermute | solution.py:525
  71.1 64.9 %collective-permute-start.1 = (bf16[768,1536]{1,0:T(8,128)(2,1)}, bf16[768,1536]{1,0:T(8,128)(2,1)}, u32[]{:S(2)}, u32[]{:S(2)}) collective-permute-start(bf16[768,1536]{1,0:T(8,128)(2,1)} %collective-permute-done.x_ref), channel_id=1, source_target_pairs={{0,2},{1,3},{2,0},{3,1},{4,5},{5,4},{6,7},{7,6},{8,10},{9,11},{10,... | collective-permute-start | bytes 7077896 | tf_op jit(solution)/shard_map/ppermute | solution.py:531
  75.1 682.6 %reduce-scatter.9.cloned.1.call-start = ((), (), s32[]{:S(2)}) async-start(), calls=%async_computation.9 | async-start | bytes 2949120 | tf_op jit(solution)/shard_map/reduce_scatter | solution.py:743
  97.7 79.1 %collective-permute-start.10 = (bf16[768,384]{1,0:T(8,128)(2,1)}, bf16[768,384]{1,0:T(8,128)(2,1)}, u32[]{:S(2)}, u32[]{:S(2)}) collective-permute-start(bf16[768,384]{1,0:T(8,128)(2,1)} %collective-permute-done.6), channel_id=1, source_target_pairs={{0,2},{1,3},{2,0},{3,1},{4,5},{5,4},{6,7},{7,6},{8,10},{9,11},{10,... | collective-permute-start | bytes 1769480 | tf_op jit(solution)/shard_map/ppermute | solution.py:531
  113.1 65.1 %collective-permute-start.8 = (bf16[768,384]{1,0:T(8,128)(2,1)}, bf16[768,384]{1,0:T(8,128)(2,1)}, u32[]{:S(2)}, u32[]{:S(2)}) collective-permute-start(bf16[768,384]{1,0:T(8,128)(2,1)} %collective-permute-done.7), channel_id=1, source_target_pairs={{0,4},{4,0},{1,5},{5,1},{2,6},{6,2},{3,7},{7,3},{8,12},{12,8},{9,1... | collective-permute-start | bytes 1769480 | tf_op jit(solution)/shard_map/ppermute | solution.py:525
  189.0 87.8 %collective-permute-start.16 = (bf16[1536,768]{1,0:T(8,128)(2,1)}, bf16[1536,768]{1,0:T(8,128)(2,1)}, u32[]{:S(2)}, u32[]{:S(2)}) collective-permute-start(bf16[1536,768]{1,0:T(8,128)(2,1)} %all-gather.8.cloned.1.call-done.w_ref.refs_9_), channel_id=1, source_target_pairs={{0,1},{1,0},{2,3},{3,2},{4,6},{5,7},{6,4},{7,5},{8,9},{9,8},{10,11... | collective-permute-start | bytes 7077896 | tf_op jit(solution)/shard_map/ppermute | solution.py:531
  212.7 69.3 %collective-permute-start.12 = (bf16[768,1536]{1,0:T(8,128)(2,1)S(1)}, bf16[768,1536]{1,0:T(8,128)(2,1)S(1)}, u32[]{:S(2)}, u32[]{:S(2)}) collective-permute-start(bf16[768,1536]{1,0:T(8,128)(2,1)S(1)} %multiply_convert_fusion), channel_id=1, source_target_pairs={{0,4},{4,0},{1,5},{5,1},{2,6},{6,2},{3,7},{7,3},{8,12},{12,8},{9,1... | collective-permute-start | bytes 7077896 | tf_op jit(solution)/shard_map/ppermute | solution.py:525
  229.0 55.4 %collective-permute-start.19 = (bf16[1536,768]{1,0:T(8,128)(2,1)}, bf16[1536,768]{1,0:T(8,128)(2,1)}, u32[]{:S(2)}, u32[]{:S(2)}) collective-permute-start(bf16[1536,768]{1,0:T(8,128)(2,1)} %collective-permute-done.15.w_ref.refs_10_), channel_id=1, source_target_pairs={{0,2},{1,3},{2,0},{3,1},{4,5},{5,4},{6,7},{7,6},{8,10},{9,11},{10,... | collective-permute-start | bytes 7077896 | tf_op jit(solution)/shard_map/ppermute | solution.py:531
  232.4 132.2 %collective-permute-start.17 = (bf16[1536,768]{1,0:T(8,128)(2,1)S(1)}, bf16[1536,768]{1,0:T(8,128)(2,1)}, u32[]{:S(2)}, u32[]{:S(2)}) collective-permute-start(bf16[1536,768]{1,0:T(8,128)(2,1)S(1)} %copy-done.2), channel_id=1, source_target_pairs={{0,2},{1,3},{2,0},{3,1},{4,5},{5,4},{6,7},{7,6},{8,10},{9,11},{10,... | collective-permute-start | bytes 7077896 | tf_op jit(solution)/shard_map/ppermute | solution.py:531
  232.6 163.9 %collective-permute-start.18 = (bf16[1536,768]{1,0:T(8,128)(2,1)}, bf16[1536,768]{1,0:T(8,128)(2,1)}, u32[]{:S(2)}, u32[]{:S(2)}) collective-permute-start(bf16[1536,768]{1,0:T(8,128)(2,1)} %all-gather.8.cloned.1.call-done.w_ref.refs_9_), channel_id=1, source_target_pairs={{0,2},{1,3},{2,0},{3,1},{4,5},{5,4},{6,7},{7,6},{8,10},{9,11},{10,... | collective-permute-start | bytes 7077896 | tf_op jit(solution)/shard_map/ppermute | solution.py:531
  276.8 103.8 %collective-permute-start.20 = (bf16[1536,768]{1,0:T(8,128)(2,1)}, bf16[1536,768]{1,0:T(8,128)(2,1)}, u32[]{:S(2)}, u32[]{:S(2)}) collective-permute-start(bf16[1536,768]{1,0:T(8,128)(2,1)} %collective-permute-done.16.w_ref.refs_11_), channel_id=1, source_target_pairs={{0,2},{1,3},{2,0},{3,1},{4,5},{5,4},{6,7},{7,6},{8,10},{9,11},{10,... | collective-permute-start | bytes 7077896 | tf_op jit(solution)/shard_map/ppermute | solution.py:531
  300.3 132.0 %collective-permute-start.34 = (bf16[1536,768]{1,0:T(8,128)(2,1)}, bf16[1536,768]{1,0:T(8,128)(2,1)}, u32[]{:S(2)}, u32[]{:S(2)}) collective-permute-start(bf16[1536,768]{1,0:T(8,128)(2,1)} %get-tuple-element.74), channel_id=1, source_target_pairs={{0,2},{1,3},{2,0},{3,1},{4,5},{5,4},{6,7},{7,6},{8,10},{9,11},{10,... | collective-permute-start | bytes 7077896 | tf_op jit(solution)/shard_map/ppermute | solution.py:531
  430.0 87.0 %collective-permute-start.22 = (f32[768,1536]{1,0:T(8,128)}, f32[768,1536]{1,0:T(8,128)}, u32[]{:S(2)}, u32[]{:S(2)}) collective-permute-start(f32[768,1536]{1,0:T(8,128)} %sum_products.7), channel_id=1, source_target_pairs={{0,4},{4,0},{1,5},{5,1},{2,6},{6,2},{3,7},{7,3},{8,12},{12,8},{9,1... | collective-permute-start | bytes 14155784 | tf_op jit(solution)/shard_map/ppermute | solution.py:525
  430.1 49.4 %collective-permute-start.38 = (bf16[1536,768]{1,0:T(8,128)(2,1)}, bf16[1536,768]{1,0:T(8,128)(2,1)}, u32[]{:S(2)}, u32[]{:S(2)}) collective-permute-start(bf16[1536,768]{1,0:T(8,128)(2,1)} %get-tuple-element.78), channel_id=1, source_target_pairs={{0,2},{1,3},{2,0},{3,1},{4,5},{5,4},{6,7},{7,6},{8,10},{9,11},{10,... | collective-permute-start | bytes 7077896 | tf_op jit(solution)/shard_map/ppermute | solution.py:531
  432.1 77.8 %collective-permute-start.33 = (bf16[1536,768]{1,0:T(8,128)(2,1)}, bf16[1536,768]{1,0:T(8,128)(2,1)}, u32[]{:S(2)}, u32[]{:S(2)}) collective-permute-start(bf16[1536,768]{1,0:T(8,128)(2,1)} %get-tuple-element.72), channel_id=1, source_target_pairs={{0,2},{1,3},{2,0},{3,1},{4,5},{5,4},{6,7},{7,6},{8,10},{9,11},{10,... | collective-permute-start | bytes 7077896 | tf_op jit(solution)/shard_map/ppermute | solution.py:531
  435.9 76.3 %collective-permute-start.35 = (bf16[1536,768]{1,0:T(8,128)(2,1)}, bf16[1536,768]{1,0:T(8,128)(2,1)}, u32[]{:S(2)}, u32[]{:S(2)}) collective-permute-start(bf16[1536,768]{1,0:T(8,128)(2,1)} %add_convert_fusion.4), channel_id=1, source_target_pairs={{0,1},{1,0},{2,3},{3,2},{4,6},{5,7},{6,4},{7,5},{8,9},{9,8},{10,11... | collective-permute-start | bytes 7077896 | tf_op jit(solution)/shard_map/ppermute | solution.py:531
  438.2 130.4 %collective-permute-start.37 = (bf16[1536,768]{1,0:T(8,128)(2,1)}, bf16[1536,768]{1,0:T(8,128)(2,1)}, u32[]{:S(2)}, u32[]{:S(2)}) collective-permute-start(bf16[1536,768]{1,0:T(8,128)(2,1)} %get-tuple-element.76), channel_id=1, source_target_pairs={{0,2},{1,3},{2,0},{3,1},{4,5},{5,4},{6,7},{7,6},{8,10},{9,11},{10,... | collective-permute-start | bytes 7077896 | tf_op jit(solution)/shard_map/ppermute | solution.py:531
  479.5 44.9 %collective-permute-start.21 = (bf16[768,1536]{1,0:T(8,128)(2,1)}, bf16[768,1536]{1,0:T(8,128)(2,1)}, u32[]{:S(2)}, u32[]{:S(2)}) collective-permute-start(bf16[768,1536]{1,0:T(8,128)(2,1)} %sum_products.5), channel_id=1, source_target_pairs={{0,4},{4,0},{1,5},{5,1},{2,6},{6,2},{3,7},{7,3},{8,12},{12,8},{9,1... | collective-permute-start | bytes 7077896 | tf_op jit(solution)/shard_map/ppermute | solution.py:525
  509.9 58.7 %collective-permute-start.39 = (bf16[1536,768]{1,0:T(8,128)(2,1)}, bf16[1536,768]{1,0:T(8,128)(2,1)}, u32[]{:S(2)}, u32[]{:S(2)}) collective-permute-start(bf16[1536,768]{1,0:T(8,128)(2,1)} %add_convert_fusion.1), channel_id=1, source_target_pairs={{0,1},{1,0},{2,3},{3,2},{4,6},{5,7},{6,4},{7,5},{8,9},{9,8},{10,11... | collective-permute-start | bytes 7077896 | tf_op jit(solution)/shard_map/ppermute | solution.py:531
  517.0 248.0 %reduce-scatter.11.cloned.1.call-start = ((), (), s32[]{:S(2)}) async-start(), calls=%async_computation.10 | async-start | bytes 2949120 | tf_op jit(solution)/shard_map/reduce_scatter | solution.py:743
  559.0 89.7 %collective-permute-start.29 = (bf16[4,192,4,384]{3,1,0,2:T(8,128)(2,1)}, bf16[4,192,4,384]{3,1,0,2:T(8,128)(2,1)}, u32[]{:S(2)}, u32[]{:S(2)}) collective-permute-start(bf16[4,192,4,384]{3,1,0,2:T(8,128)(2,1)} %pad_maximum_fusion.3), channel_id=1, source_target_pairs={{0,4},{4,0},{1,5},{5,1},{2,6},{6,2},{3,7},{7,3},{8,12},{12,8},{9,1... | collective-permute-start | bytes 7077896 | tf_op jit(solution)/shard_map/ppermute | solution.py:525
  574.0 209.0 %reduce-scatter.7.cloned.1.call-start = ((), (), s32[]{:S(2)}) async-start(), calls=%async_computation.8 | async-start | bytes 737280 | tf_op jit(solution)/shard_map/reduce_scatter | solution.py:706
  656.8 131.7 %collective-permute-start.26 = (bf16[768,1536]{1,0:T(8,128)(2,1)}, bf16[768,1536]{1,0:T(8,128)(2,1)}, u32[]{:S(2)}, u32[]{:S(2)}) collective-permute-start(bf16[768,1536]{1,0:T(8,128)(2,1)} %convolution_convert_fusion.4), channel_id=1, source_target_pairs={{0,2},{1,3},{2,0},{3,1},{4,5},{5,4},{6,7},{7,6},{8,10},{9,11},{10,... | collective-permute-start | bytes 7077896 | tf_op jit(solution)/shard_map/ppermute | solution.py:531
  660.1 81.3 %collective-permute-start.30 = (bf16[768,384]{1,0:T(8,128)(2,1)S(1)}, bf16[768,384]{1,0:T(8,128)(2,1)S(1)}, u32[]{:S(2)}, u32[]{:S(2)}) collective-permute-start(bf16[768,384]{1,0:T(8,128)(2,1)S(1)} %bitcast.143), channel_id=1, source_target_pairs={{0,2},{1,3},{2,0},{3,1},{4,5},{5,4},{6,7},{7,6},{8,10},{9,11},{10,... | collective-permute-start | bytes 1769480 | tf_op jit(solution)/shard_map/ppermute | solution.py:531
  683.3 58.1 %collective-permute-start.32 = (bf16[768,384]{1,0:T(8,128)(2,1)S(1)}, bf16[768,384]{1,0:T(8,128)(2,1)S(1)}, u32[]{:S(2)}, u32[]{:S(2)}) collective-permute-start(bf16[768,384]{1,0:T(8,128)(2,1)S(1)} %fusion.15), channel_id=1, source_target_pairs={{0,1},{1,0},{2,3},{3,2},{4,6},{5,7},{6,4},{7,5},{8,9},{9,8},{10,11... | collective-permute-start | bytes 1769480 | tf_op jit(solution)/shard_map/ppermute | solution.py:531
  685.4 103.1 %collective-permute-start.28 = (bf16[768,1536]{1,0:T(8,128)(2,1)}, bf16[768,1536]{1,0:T(8,128)(2,1)}, u32[]{:S(2)}, u32[]{:S(2)}) collective-permute-start(bf16[768,1536]{1,0:T(8,128)(2,1)} %add_convert_fusion.6), channel_id=1, source_target_pairs={{0,1},{1,0},{2,3},{3,2},{4,6},{5,7},{6,4},{7,5},{8,9},{9,8},{10,11... | collective-permute-start | bytes 7077896 | tf_op jit(solution)/shard_map/ppermute | solution.py:531
  742.5 101.0 %reduce-scatter.5.cloned.1.call-start = ((), (), s32[]{:S(2)}) async-start(), calls=%async_computation.7 | async-start | bytes 2654208 | tf_op jit(solution)/shard_map/reduce_scatter | solution.py:731
  (45 other events, 557.5 us)
Sparse Core Ops, SparseCore 0:
  10.9 47.4 all-gather.3
  60.0 48.8 all-gather.5
  110.4 48.7 all-gather.7
  517.1 54.2 reduce-scatter.8
  574.1 54.4 reduce-scatter.10
  742.6 40.3 reduce-scatter.6
  785.3 35.5 reduce-scatter.4
